TPU v7x, 128 devices: a whole 4x4x4 slice. The times are simulated.
128 devices in a mesh: blk: 16 (over z, y_lo, core), lat: 8 (over x, y_hi).
Axes of the slice: x: 4, y: 4 (y_hi: 2, y_lo: 2; y = y_hi * 2 + y_lo), z: 4, core: 2. Of those that a mesh axis runs over, the one named last changes fastest.
Arguments:
- displacement: float32 [2, 3, 1272960], P(None, None, ('blk', 'lat')), may hold values from -5 to 5, as said below
- velocity: float32 [2, 3, 1272960], P(None, None, ('blk', 'lat')), may hold values from -2.5 to 2.5, as said below
- lumped_mass: float32 [1272960], P(('blk', 'lat')), may hold values from 0.25 to 225, as said below
- shear_modulus: float32 [125, 16384], P(None, ('blk', 'lat')), may hold values from 0.3 to 1
- lame_modulus: float32 [125, 16384], P(None, ('blk', 'lat')), may hold values from 0.3 to 1
- adjoint_sources: bfloat16 [32, 3, 1272960], P(None, None, ('blk', 'lat')), may hold values from -24 to 24
- node_numbers: int32 [125, 16384], P(None, ('blk', 'lat')), may hold values from 0 to 9944, as said below
- event_frequency: int32 [2, 32], replicated, may hold values from 0 to 31, each once within a row
Outputs:
- final_displacement: float32 [2, 3, 1272960], P(None, None, ('blk', 'lat'))
- final_velocity: float32 [2, 3, 1272960], P(None, None, ('blk', 'lat'))
- strain_spectrum: float32 [2, 32, 2, 5, 16384], P(None, None, None, None, ('blk', 'lat'))
Inputs may be any that keep to these rules, and one draw needn't show every extreme that they name: `node_numbers`: each device's columns number its 9945 nodes, each node once across its elements' shared points. A device's element at grid place (ex, ey, ez), 0 <= ex < 2, 0 <= ey < 4, 0 <= ez < 16, touches a neighbour's face when ex or ey is at an end of its range; the first 128 columns of each device are these elements in the order of ex * 4 * 16 + ey * 16 + ez, the remaining columns the other elements in the same order. `event_frequency`: each row gives the events of one supershot distinct frequencies. `displacement`: all copies of a mesh node hold equal values. `velocity`: all copies of a mesh node hold equal values. `lumped_mass`: all copies of a mesh node hold equal values, the mass assembled over all elements of the mesh.
All inputs are finite; a program needn't handle non-finite values.
Results may differ from a plain program's by a relative error of at most 0.0034.
Values sent between devices are 32-bit elements; how exact they have to be, the bound alone decides.
No kernel may reach another device: no remote copies, remote signals or barrier semaphores. Data moves between devices by JAX's collectives and lax.ppermute only.
A program may use at most 128 MiB of HBM per device.

v0:
```python
import math

import jax
import jax.numpy as jnp
import numpy as np
from jax import lax
from jax.experimental import pallas as pl
from jax.experimental.pallas import tpu as pltpu
from jax.sharding import PartitionSpec as P


EXB = 2
EYL = 4
EZ = 16
NFREQ = 32
EVENTS = 32
STEP_TOTAL = 4
NXN = 9
NYN = 17
NODES_DEV = 9945
NODE_BLOCKS = 78
LINE = 72
COMPS = 40
SLOTS = 4


bf16 = jnp.bfloat16
f32 = jnp.float32


def gll_numpy():
    points = np.array([-1.0, -math.sqrt(3.0 / 7.0), 0.0, math.sqrt(3.0 / 7.0), 1.0])
    weights = np.array([0.1, 49.0 / 90.0, 32.0 / 45.0, 49.0 / 90.0, 0.1])
    products = np.ones(5)
    for target in range(5):
        for source in range(5):
            if source != target:
                products[target] *= points[target] - points[source]
    derivative = np.zeros((5, 5))
    for target in range(5):
        for source in range(5):
            if source != target:
                derivative[target, source] = (
                    products[target] / products[source] / (points[target] - points[source])
                )
        derivative[target, target] = -np.sum(derivative[target])
    cube = weights[:, None, None] * weights[None, :, None] * weights[None, None, :] / 8.0
    return derivative, cube.reshape(125)


def split_np(matrix):
    high = np.asarray(matrix, np.float32).astype(bf16)
    low = (matrix - high.astype(np.float64)).astype(np.float32).astype(bf16)
    return high, low


def operator_tables():
    derivative, cube = gll_numpy()
    eye = np.eye(5)
    parts = [
        2.0 * np.kron(np.kron(derivative, eye), eye),
        2.0 * np.kron(np.kron(eye, derivative), eye),
        2.0 * np.kron(np.kron(eye, eye), derivative),
    ]
    forward = np.zeros((3, 128, 128))
    backward = np.zeros((128, 3, 128))
    for d in range(3):
        forward[d, :125, :125] = parts[d]
        forward[d, 125, :125] = cube @ parts[d]
        backward[:125, d, :125] = parts[d].T
    fwd_high, fwd_low = split_np(forward.reshape(384, 128))
    bwd_high, bwd_low = split_np(backward.reshape(128, 384))
    gradient = np.concatenate([fwd_high, fwd_high, fwd_low], axis=1)
    divergence = np.concatenate([bwd_high, bwd_high, bwd_low], axis=1)
    weight = np.zeros((128, 128), np.float32)
    weight[:125] = cube[:, None]
    return gradient, divergence, weight


def frequency_tables():
    omega = np.pi * (1.0 + np.arange(NFREQ)) / (NFREQ + 1.0)
    times = 1.0 + np.arange(STEP_TOTAL)
    angles = omega[:, None] * times[None, :]
    pulses = np.zeros((8, NFREQ), np.float32)
    pulses[:STEP_TOTAL] = np.cos(angles).T
    pulses = pulses.astype(bf16)
    spectra = np.concatenate([np.cos(angles), -np.sin(angles)], axis=0)
    wide = np.einsum("rk,mn->rmkn", spectra, np.eye(10)).reshape(64 * 10, STEP_TOTAL * 10)
    high, low = split_np(wide)
    zero = np.zeros((640, 8), high.dtype)
    return pulses, np.concatenate([high, high, low, zero], axis=1)


def split2(values):
    high = values.astype(bf16)
    low = (values - high.astype(f32)).astype(bf16)
    return high, low


def vmem():
    return pl.BlockSpec(memory_space=pltpu.VMEM)


def smem():
    return pl.BlockSpec(memory_space=pltpu.SMEM)


def for_nodes(numbers, columns_hbm, chunks, sems, pair_places, visit):
    def fetch(pair, slot):
        row = 25 * lax.shift_right_logical(pair, 2) + 5 * (pair & 3)
        return pltpu.make_async_copy(
            columns_hbm.at[pl.ds(row, 4)], chunks.at[slot], sems.at[slot]
        )

    for slot in range(SLOTS):
        fetch(jnp.int32(slot), slot).start()

    def some_pairs(index, carry):
        for slot in range(SLOTS):
            pair = SLOTS * index + slot
            fetch(pair, slot).wait()
            a, b = lax.shift_right_logical(pair, 2), pair & 3
            for c in range(4):
                places = pair_places(a, b, c)
                for ex in range(EXB):
                    for ey in range(EYL):
                        for ez in range(EZ):
                            node = chunks[slot, c, 0, 64 * ex + 16 * ey + ez]
                            visit(places, c, ex, ey, ez, node)

            @pl.when(index < 16 // SLOTS - 1)
            def _():
                fetch(pair + SLOTS, slot).start()

        return carry

    lax.fori_loop(0, 16 // SLOTS, some_pairs, 0)

    def far_line(ix, iy, c_count):
        ex = jnp.minimum(lax.shift_right_logical(ix, 2), EXB - 1)
        ey = jnp.minimum(lax.shift_right_logical(iy, 2), EYL - 1)
        a, b = ix - 4 * ex, iy - 4 * ey
        start = 3200 * a + 640 * b + 64 * ex + 16 * ey
        for c in range(5 - c_count, 5) if c_count == 1 else range(c_count):
            places = pair_places(a, b, c)
            for ez in range(EZ - 1 if c == 4 else 0, EZ):
                visit(places, c, ex, ey, ez, numbers[start + 128 * c + ez])

    def last_plane(iy, carry):
        far_line(jnp.int32(NXN - 1), iy, 4)
        return carry

    lax.fori_loop(0, NYN, last_plane, 0)

    def last_row(ix, carry):
        far_line(ix, jnp.int32(NYN - 1), 4)
        return carry

    lax.fori_loop(0, NXN - 1, last_row, 0)

    def top(ix, carry):
        for iy in range(NYN):
            far_line(ix, jnp.int32(iy), 1)
        return carry

    lax.fori_loop(0, NXN, top, 0)


def for_blocks(count, unroll, body):
    def group(index, carry):
        for part in range(unroll):
            body(index * unroll + part)
        return carry

    lax.fori_loop(0, count // unroll, group, 0)


def gather_kernel(
    columns_hbm,
    numbers_hbm,
    sources_hbm,
    displacement_hbm,
    velocity_hbm,
    mass_hbm,
    shear_hbm,
    lame_hbm,
    weight_hbm,
    pulses_hbm,
    frequency_hbm,
    force_out,
    motion_out,
    speed_out,
    inverse_out,
    shear_out,
    lame_out,
    mixing,
    rows,
    table,
    lines,
    numbers,
    sources,
    displacement,
    velocity,
    mass,
    shear,
    lame,
    weight,
    pulses,
    frequency,
    sems,
    chunks,
    chunk_sems,
):
    copies = [
        pltpu.make_async_copy(source, target, sems.at[position])
        for position, (source, target) in enumerate(
            (
                (frequency_hbm, frequency),
                (pulses_hbm, pulses),
                (sources_hbm, sources),
                (displacement_hbm, displacement),
                (velocity_hbm, velocity),
                (mass_hbm, mass),
                (numbers_hbm, numbers),
                (shear_hbm, shear),
                (lame_hbm, lame),
                (weight_hbm, weight),
            )
        )
    ]
    for copy in copies:
        copy.start()
    for copy in copies[0:2]:
        copy.wait()
    index = lax.broadcasted_iota(jnp.int32, (NFREQ, EVENTS), 0)
    mixing[...] = jnp.zeros((24, 3 * EVENTS), f32)
    for s in range(2):
        chosen = (frequency[s : s + 1, :] == index).astype(f32).astype(bf16)
        wavelet = jnp.dot(pulses[...], chosen, preferred_element_type=f32)
        for k in range(STEP_TOTAL):
            for q in range(3):
                row = 6 * k + 2 * q + s
                mixing[row : row + 1, EVENTS * q : EVENTS * (q + 1)] = wavelet[k : k + 1]
    for copy in copies[3:6]:
        copy.wait()
    for q in range(3):
        rows[24 + 2 * q : 26 + 2 * q, 0:NODES_DEV] = displacement[q]
        rows[32 + 2 * q : 34 + 2 * q, 0:NODES_DEV] = velocity[q]
    rows[38:39, 0:NODES_DEV] = mass[...].reshape(1, NODES_DEV)
    copies[2].wait()
    flat = sources[...].reshape(3 * EVENTS, NODES_DEV)
    rows[0:24, 0:NODES_DEV] = jnp.dot(
        mixing[...].astype(bf16), flat, preferred_element_type=f32
    )

    def transpose_block(block):
        start = pl.multiple_of(block * 128, 128)
        block_rows = rows[:, pl.ds(start, 128)]
        filler = jnp.zeros((128 - 3 * COMPS, 128), f32)
        table[pl.ds(start, 128), :] = jnp.concatenate(
            [block_rows, block_rows, block_rows, filler], axis=0
        ).T

    for_blocks(NODE_BLOCKS, 6, transpose_block)
    for copy in copies[6:]:
        copy.wait()

    def line_places(a, b, c):
        return (a * NYN + b) * LINE + c

    def gather_node(place, c, ex, ey, ez, node):
        del c
        at = place + ((4 * ex * NYN + 4 * ey) * LINE + 4 * ez)
        lines[pl.ds(at, 1), :] = table[pl.ds(node, 1), :]

    for_nodes(numbers, columns_hbm, chunks, chunk_sems, line_places, gather_node)

    lanes = lanes_of(128)

    def element_rows(pair):
        a = lax.shift_right_logical(pair * 13, 6)
        b = pair - 5 * a
        for group in ((0, 1, 2), (3, 4)):
            mixed = None
            for position, c in reversed(list(enumerate(group))):
                pieces = []
                for ex in range(EXB):
                    for ey in range(EYL):
                        line = (4 * ex + a) * NYN + 4 * ey + b
                        pieces.append(lines[pl.ds(line * LINE + c, EZ, stride=4), :])
                whole = jnp.concatenate(pieces, axis=0)
                if mixed is None:
                    mixed = whole
                else:
                    mixed = jnp.where(lanes < COMPS * (position + 1), whole, mixed)
            turned = mixed.T
            for position, c in enumerate(group):
                point = pair * 5 + c
                base = COMPS * position
                force_out[pl.ds(point, 24, stride=128), :] = turned[base : base + 24]
                motion_out[pl.ds(point, 6, stride=128), :] = turned[base + 24 : base + 30]
                speed_out[pl.ds(point, 6, stride=128), :] = turned[base + 32 : base + 38]
                inverse_out[pl.ds(point, 1), :] = 1.0 / turned[base + 38 : base + 39]

    for_blocks(25, 1, element_rows)
    for point in range(125, 128):
        force_out[pl.ds(point, 24, stride=128), :] = jnp.zeros((24, 128), f32)
        motion_out[pl.ds(point, 6, stride=128), :] = jnp.zeros((6, 128), f32)
        speed_out[pl.ds(point, 6, stride=128), :] = jnp.zeros((6, 128), f32)
    inverse_out[125:128, :] = jnp.zeros((3, 128), f32)
    shear_out[0:125, :] = shear[...] * weight[0:125, :]
    shear_out[125:128, :] = jnp.zeros((3, 128), f32)
    lame_out[0:125, :] = lame[...] * weight[0:125, :]
    lame_out[125:128, :] = jnp.zeros((3, 128), f32)


def lanes_of(count):
    return lax.broadcasted_iota(jnp.int32, (count, 128), 1)


def balance_of(motion, force, step, shear, lame, gradient, divergence, balance, integral):
    fields = jnp.concatenate([motion[128 * j : 128 * j + 128, :] for j in range(6)], axis=1)
    high, low = split2(fields)
    grads = jnp.dot(
        gradient[...], jnp.concatenate([high, low, high], axis=0), preferred_element_type=f32
    )

    def grad(d, q, s):
        j = 2 * q + s
        return grads[128 * d : 128 * d + 128, 128 * j : 128 * j + 128]

    mu = shear[...]
    lam = lame[...]
    stress = {}
    for s in range(2):
        pressure = lam * (grad(0, 0, s) + grad(1, 1, s) + grad(2, 2, s))
        for d in range(3):
            for q in range(d, 3):
                value = mu * (grad(d, q, s) + grad(q, d, s))
                if q == d:
                    value = value + pressure
                stress[d, q, s] = stress[q, d, s] = split2(value)
    highs, lows = (
        jnp.concatenate(
            [
                jnp.concatenate([stress[d, j // 2, j % 2][part] for j in range(6)], axis=1)
                for d in range(3)
            ],
            axis=0,
        )
        for part in range(2)
    )
    internal = jnp.dot(
        divergence[...], jnp.concatenate([highs, lows, highs], axis=0), preferred_element_type=f32
    )
    for j in range(6):
        balance[128 * j : 128 * j + 128, :] = internal[:, 128 * j : 128 * j + 128]

    def weighted(d, q):
        row = 128 * d + 125
        return jnp.concatenate(
            [grads[row : row + 1, 128 * j : 128 * j + 128] for j in (2 * q, 2 * q + 1)], axis=0
        )

    third = (weighted(0, 0) + weighted(1, 1) + weighted(2, 2)) / 3.0
    integral[0:2, :] = weighted(0, 0) - third
    integral[2:4, :] = weighted(1, 1) - third
    integral[4:6, :] = 0.5 * (weighted(0, 1) + weighted(1, 0))
    integral[6:8, :] = 0.5 * (weighted(0, 2) + weighted(2, 0))
    integral[8:10, :] = 0.5 * (weighted(1, 2) + weighted(2, 1))

    lane = lanes_of(25)
    keep = lane % 16
    for j in range(6):
        base = 128 * j
        first = balance[pl.ds(base, 25, stride=5), :]
        last = balance[pl.ds(base + 4, 25, stride=5), :]
        balance[pl.ds(base, 25, stride=5), :] = first + jnp.where(
            keep != 0, pltpu.roll(last, 1, 1), 0.0
        )
        balance[pl.ds(base + 4, 25, stride=5), :] = last + jnp.where(
            keep != 15, pltpu.roll(first, 127, 1), 0.0
        )
    side = lanes_of(5) % 64
    for j in range(6):
        for a in range(5):
            base = 128 * j + 25 * a
            first = balance[base : base + 5, :]
            last = balance[base + 20 : base + 25, :]
            balance[base : base + 5, :] = first + jnp.where(
                side >= 16, pltpu.roll(last, 16, 1), 0.0
            )
            balance[base + 20 : base + 25, :] = last + jnp.where(
                side < 48, pltpu.roll(first, 112, 1), 0.0
            )
    for j in range(6):
        base = 128 * j
        first = balance[base : base + 25, :]
        last = balance[base + 100 : base + 125, :]
        balance[base : base + 25, :] = first + jnp.where(
            lane >= 64, pltpu.roll(last, 64, 1), 0.0
        )
        balance[base + 100 : base + 125, :] = last + jnp.where(
            lane < 64, pltpu.roll(first, 64, 1), 0.0
        )
    balance[...] = force[768 * step : 768 * step + 768, :] - balance[...]


def pack_cycle(balance, side, even_out, odd_out):
    lane = lanes_of(25)
    even = (side[0] & 1) == 0
    for g in range(3):
        near, far = 128 * g, 128 * (g + 3)
        low = jnp.where(
            lane < 64, balance[near : near + 25, :], pltpu.roll(balance[far : far + 25, :], 64, 1)
        )
        up = jnp.where(
            lane < 64,
            pltpu.roll(balance[near + 100 : near + 125, :], 64, 1),
            balance[far + 100 : far + 125, :],
        )
        even_out[32 * g : 32 * g + 25, :] = jnp.where(even, up, low)
        odd_out[32 * g : 32 * g + 25, :] = jnp.where(even, low, up)


def add_cycle(balance, side, even_in, odd_in):
    lane = lanes_of(25)
    even = (side[0] & 1) == 0
    for g in range(3):
        near, far = 128 * g, 128 * (g + 3)
        first = even_in[32 * g : 32 * g + 25, :]
        second = odd_in[32 * g : 32 * g + 25, :]
        up = jnp.where(even, first, second)
        low = jnp.where(even, second, first)
        balance[near : near + 25, :] += jnp.where(lane < 64, low, 0.0)
        balance[far : far + 25, :] += jnp.where(lane < 64, pltpu.roll(low, 64, 1), 0.0)
        balance[near + 100 : near + 125, :] += jnp.where(lane >= 64, pltpu.roll(up, 64, 1), 0.0)
        balance[far + 100 : far + 125, :] += jnp.where(lane >= 64, up, 0.0)


def turn(values, slots):
    return values if slots % 8 == 0 else pltpu.roll(values, (16 * slots) % 128, 1)


def pack_lat(balance, side, even_out, odd_out):
    slot = lanes_of(5) // 16 % 4
    even = (side[0] & 1) == 0
    for g in range(2):
        for a in range(5):
            low = jnp.zeros((5, 128), f32)
            up = jnp.zeros((5, 128), f32)
            for t in range(4):
                j = 4 * g + t
                if j >= 6:
                    break
                base = 128 * j + 25 * a
                low = jnp.where(slot == t, turn(balance[base : base + 5, :], t), low)
                up = jnp.where(slot == t, turn(balance[base + 20 : base + 25, :], t - 3), up)
            at = 32 * g + 5 * a
            even_out[at : at + 5, :] = jnp.where(even, up, low)
            odd_out[at : at + 5, :] = jnp.where(even, low, up)


def add_lat(balance, side, even_in, odd_in):
    slot = lanes_of(5) // 16 % 4
    even = (side[0] & 1) == 0
    for g in range(2):
        for a in range(5):
            at = 32 * g + 5 * a
            first = even_in[at : at + 5, :]
            second = odd_in[at : at + 5, :]
            up = jnp.where(even, first, second)
            low = jnp.where(even, second, first)
            for t in range(4):
                j = 4 * g + t
                if j >= 6:
                    break
                base = 128 * j + 25 * a
                balance[base : base + 5, :] += jnp.where(slot == 0, turn(low, -t), 0.0)
                balance[base + 20 : base + 25, :] += jnp.where(slot == 3, turn(up, 3 - t), 0.0)


def first_kernel(
    blk, motion, force, shear, lame, gradient, divergence, balance, integral, even_out, odd_out
):
    balance_of(motion, force, 0, shear, lame, gradient, divergence, balance, integral)
    pack_cycle(balance, blk, even_out, odd_out)


def middle_kernel(blk, lat, old, even_in, odd_in, balance, even_out, odd_out):
    balance[...] = old[...]
    add_cycle(balance, blk, even_in, odd_in)
    pack_lat(balance, lat, even_out, odd_out)


def advance(lat, old, even_in, odd_in, inverse, motion_in, speed_in, motion, speed, balance):
    balance[...] = old[...]
    add_lat(balance, lat, even_in, odd_in)
    scale = inverse[...]
    for j in range(6):
        part = slice(128 * j, 128 * j + 128)
        now = speed_in[part, :] + balance[part, :] * scale
        speed[part, :] = now
        motion[part, :] = motion_in[part, :] + now


def make_step_kernel(step):
    def step_kernel(
        blk,
        lat,
        old,
        even_in,
        odd_in,
        inverse,
        motion_in,
        speed_in,
        force,
        shear,
        lame,
        gradient,
        divergence,
        balance,
        motion,
        speed,
        integral,
        even_out,
        odd_out,
    ):
        advance(lat, old, even_in, odd_in, inverse, motion_in, speed_in, motion, speed, balance)
        balance_of(motion, force, step, shear, lame, gradient, divergence, balance, integral)
        pack_cycle(balance, blk, even_out, odd_out)

    return step_kernel


def last_kernel(
    columns_hbm,
    numbers,
    lat,
    old,
    even_in,
    odd_in,
    inverse,
    motion_in,
    speed_in,
    motion_out,
    speed_out,
    balance,
    state,
    points,
    table,
    chunks,
    chunk_sems,
):
    advance(
        lat,
        old,
        even_in,
        odd_in,
        inverse,
        motion_in,
        speed_in,
        state.at[0:768, :],
        state.at[768:1536, :],
        balance,
    )

    def point_rows(group):
        values = jnp.concatenate(
            [state[pl.ds(group * 8 + part, 16, stride=128), :] for part in range(8)], axis=0
        )
        start = pl.multiple_of(group * 128, 128)
        points[pl.ds(start, 128), :] = values.T

    for_blocks(16, 4, point_rows)
    part_of = lanes_of(1) // 16

    def point_places(a, b, c):
        point = 25 * a + 5 * b + c
        return lax.shift_right_logical(point, 3) * 128, part_of == (point & 7)

    def scatter_node(places, c, ex, ey, ez, node):
        del c
        at = places[0] + (64 * ex + 16 * ey + ez)
        table[pl.ds(node, 1), :] = jnp.where(places[1], points[pl.ds(at, 1), :], 0.0)

    for_nodes(numbers, columns_hbm, chunks, chunk_sems, point_places, scatter_node)

    def turned(start):
        values = table[pl.ds(start, 128), :].T
        total = values[0:16]
        for part in range(1, 8):
            total = total + values[16 * part : 16 * part + 16]
        return total

    def transpose_block(block):
        start = pl.multiple_of(block * 128, 128)
        values = turned(start)
        for q in range(3):
            motion_out[q, :, pl.ds(start, 128)] = values[2 * q : 2 * q + 2]
            speed_out[q, :, pl.ds(start, 128)] = values[6 + 2 * q : 8 + 2 * q]

    for_blocks(NODE_BLOCKS - 1, 7, transpose_block)
    start = 128 * (NODE_BLOCKS - 1)
    rest = NODES_DEV - start
    values = turned(start)
    for q in range(3):
        motion_out[q, :, start:NODES_DEV] = values[2 * q : 2 * q + 2, 0:rest]
        speed_out[q, :, start:NODES_DEV] = values[6 + 2 * q : 8 + 2 * q, 0:rest]


def spectrum_kernel(wide, first, second, third, fourth, out):
    values = jnp.concatenate([part[...] for part in (first, second, third, fourth)], axis=0)
    high, low = split2(values)
    zero = jnp.zeros((8, 128), bf16)
    out[...] = jnp.dot(
        wide[...], jnp.concatenate([high, low, high, zero], axis=0), preferred_element_type=f32
    )


def kept(*extent):
    return pltpu.VMEM(extent, f32)


def hold(*arrays):
    return tuple(pltpu.with_memory_space_constraint(array, pltpu.VMEM) for array in arrays)


def exchange(axis, odd, even, odd_pairs, even_pairs):
    odd = lax.ppermute(odd, axis, odd_pairs)
    even = lax.ppermute(even, axis, even_pairs)
    return odd, even


def limit(mebibytes):
    return pltpu.CompilerParams(vmem_limit_bytes=mebibytes * 1024 * 1024)


def local(
    displacement,
    velocity,
    lumped_mass,
    shear_modulus,
    lame_modulus,
    adjoint_sources,
    node_numbers,
    event_frequency,
):
    gradient, divergence, weight = (jnp.asarray(table) for table in operator_tables())
    pulses, wide = frequency_tables()
    blk = lax.axis_index("blk").astype(jnp.int32).reshape(1)
    lat = lax.axis_index("lat").astype(jnp.int32).reshape(1)
    numbers = node_numbers.reshape(125 * 128)
    columns = node_numbers.reshape(125, 1, 128)
    blk_count = lax.axis_size("blk")
    lat_count = lax.axis_size("lat")
    cycle_even = [(i, i ^ 1) for i in range(blk_count)]
    cycle_odd = [(i, (((i + 1) ^ 1) - 1) % blk_count) for i in range(blk_count)]
    lat_even = [(i, i ^ 1) for i in range(lat_count)]
    lat_odd = [(i, ((i + 1) ^ 1) - 1) for i in range(1, lat_count - 1)]

    force, motion, speed, inverse, shear, lame = pl.pallas_call(
        gather_kernel,
        out_shape=(
            kept(24 * 128, 128),
            kept(768, 128),
            kept(768, 128),
            kept(128, 128),
            kept(128, 128),
            kept(128, 128),
        ),
        in_specs=[pl.BlockSpec(memory_space=pltpu.HBM)] * 11,
        out_specs=[vmem()] * 6,
        scratch_shapes=[
            pltpu.VMEM((24, 3 * EVENTS), f32),
            pltpu.VMEM((COMPS, NODE_BLOCKS * 128), f32),
            pltpu.VMEM((NODE_BLOCKS * 128, 128), f32),
            pltpu.VMEM((NXN * NYN * LINE, 128), f32),
            pltpu.SMEM((125 * 128,), jnp.int32),
            pltpu.VMEM((3, EVENTS, NODES_DEV), bf16),
            pltpu.VMEM((3, 2, NODES_DEV), f32),
            pltpu.VMEM((3, 2, NODES_DEV), f32),
            pltpu.VMEM((NODES_DEV,), f32),
            pltpu.VMEM((125, 128), f32),
            pltpu.VMEM((125, 128), f32),
            pltpu.VMEM((128, 128), f32),
            pltpu.VMEM((8, NFREQ), bf16),
            pltpu.VMEM((2, EVENTS), jnp.int32),
            pltpu.SemaphoreType.DMA((10,)),
            pltpu.SMEM((SLOTS, 4, 1, 128), jnp.int32),
            pltpu.SemaphoreType.DMA((SLOTS,)),
        ],
        compiler_params=limit(24),
        name="gather",
    )(
        *(
            pltpu.with_memory_space_constraint(array, pltpu.HBM)
            for array in (
                columns,
                numbers,
                adjoint_sources.transpose(1, 0, 2),
                displacement.transpose(1, 0, 2),
                velocity.transpose(1, 0, 2),
                lumped_mass,
                shear_modulus,
                lame_modulus,
                weight,
                jnp.asarray(pulses),
                event_frequency,
            )
        )
    )
    force, motion, speed, inverse, shear, lame, gradient, divergence = hold(
        force, motion, speed, inverse, shear, lame, gradient, divergence
    )
    balance_shape, integral_shape = kept(768, 128), kept(10, 128)
    cycle_shape, lat_shape = kept(96, 128), kept(64, 128)
    integrals = []
    for step in range(STEP_TOTAL):
        if step == 0:
            balance, integral, even, odd = pl.pallas_call(
                first_kernel,
                out_shape=(balance_shape, integral_shape, cycle_shape, cycle_shape),
                in_specs=[smem()] + [vmem()] * 6,
                out_specs=[vmem()] * 4,
                compiler_params=limit(8),
                name="first",
            )(blk, motion, force, shear, lame, gradient, divergence)
        else:
            balance, motion, speed, integral, even, odd = pl.pallas_call(
                make_step_kernel(step),
                out_shape=(
                    balance_shape,
                    balance_shape,
                    balance_shape,
                    integral_shape,
                    cycle_shape,
                    cycle_shape,
                ),
                in_specs=[smem()] * 2 + [vmem()] * 11,
                out_specs=[vmem()] * 6,
                compiler_params=limit(8),
                name="step",
            )(
                blk,
                lat,
                balance,
                even,
                odd,
                inverse,
                motion,
                speed,
                force,
                shear,
                lame,
                gradient,
                divergence,
            )
            motion, speed = hold(motion, speed)
        integrals.append(integral)
        odd, even = exchange("blk", odd, even, cycle_odd, cycle_even)
        balance, even, odd = pl.pallas_call(
            middle_kernel,
            out_shape=(balance_shape, lat_shape, lat_shape),
            in_specs=[smem()] * 2 + [vmem()] * 3,
            out_specs=[vmem()] * 3,
            compiler_params=limit(8),
            name="middle",
        )(blk, lat, *hold(balance, even, odd))
        odd, even = exchange("lat", odd, even, lat_odd, lat_even)
        balance, even, odd = hold(balance, even, odd)
    spectrum = pl.pallas_call(
        spectrum_kernel,
        out_shape=jax.ShapeDtypeStruct((640, 128), f32),
        in_specs=[vmem()] * 5,
        out_specs=vmem(),
        compiler_params=limit(8),
        name="spectrum",
    )(*hold(jnp.asarray(wide), *integrals))
    nodal = jax.ShapeDtypeStruct((3, 2, NODES_DEV), f32)
    final_motion, final_speed = pl.pallas_call(
        last_kernel,
        out_shape=(nodal, nodal),
        in_specs=[pl.BlockSpec(memory_space=pltpu.HBM)] + [smem()] * 2 + [vmem()] * 6,
        out_specs=[vmem()] * 2,
        scratch_shapes=[
            pltpu.VMEM((768, 128), f32),
            pltpu.VMEM((2048, 128), f32),
            pltpu.VMEM((16 * 128, 128), f32),
            pltpu.VMEM((NODE_BLOCKS * 128, 128), f32),
            pltpu.SMEM((SLOTS, 4, 1, 128), jnp.int32),
            pltpu.SemaphoreType.DMA((SLOTS,)),
        ],
        compiler_params=limit(24),
        name="last",
    )(
        pltpu.with_memory_space_constraint(columns, pltpu.HBM),
        numbers,
        lat,
        balance,
        even,
        odd,
        inverse,
        motion,
        speed,
    )
    return (
        final_motion.transpose(1, 0, 2),
        final_speed.transpose(1, 0, 2),
        spectrum.reshape(2, NFREQ, 5, 2, 128).transpose(0, 1, 3, 2, 4),
    )


def solution(mesh):
    nodes = P(None, None, ("blk", "lat"))
    columns = P(None, ("blk", "lat"))
    return jax.shard_map(
        local,
        mesh=mesh,
        in_specs=(nodes, nodes, P(("blk", "lat")), columns, columns, nodes, columns, P()),
        out_specs=(nodes, nodes, P(None, None, None, None, ("blk", "lat"))),
        check_vma=False,
    )
```

profile of v0, /device:TPU:6, one launch (start us, length us, event | category | flops | bytes accessed | tf_op | source)
XLA Modules:
  0.0 103.8 jit_solution(13962256007135089574)
XLA Ops:
  0.6 0.0 copy-start
  0.6 0.0 copy-start.1
  0.7 1.6 %reshape.21.columns_hbm = s32[125,1,128]{2,1,0:T(1,128)} reshape(s32[125,128]{1,0:T(8,128)} %param.19) | data formatting | bytes 128000 | tf_op jit(solution)/shard_map/reshape | solution.py:654
  2.2 15.1 %gather.1 = (f32[3072,128]{1,0:T(8,128)S(1)}, f32[768,128]{1,0:T(8,128)S(1)}, f32[768,128]{1,0:T(8,128)S(1)}, f32[128,128]{1,0:T(8,128)S(1)}, f32[128,128]{1,0:T(8,128)S(1)}, /*index=5*/f32[128,128]{1,0:T(8,128)S(1)}) custom-call(s32[125,1,128]{2,1,0:T(1,128)} %reshape.21.columns_hbm, s32[16000]{0:T(1024)} %bitcast.11, bf16[3,32,9945]{2,1,0:T(8,128)(2,1)} %bitcast.13, ...), custom_call_target="tpu_custom_call" | custom-call | tf_op jit(solution)/shard_map/gather/pallas_call | solution.py:662
  17.3 0.0 copy-done
  17.3 0.0 copy-done.1
  17.3 2.3 %first.1 = (f32[768,128]{1,0:T(8,128)S(1)}, f32[10,128]{1,0:T(8,128)S(1)}, f32[96,128]{1,0:T(8,128)}, f32[96,128]{1,0:T(8,128)}) custom-call(s32[1]{0:T(128)} %bitcast.2.blk, f32[768,128]{1,0:T(8,128)S(1)} %get-tuple-element.45.motion.motion_in, f32[3072,128]{1,0:T(8,128)S(1)} %get-tuple-element.46.force, f32[128,128]{1,0:T(8,128)S(1)} %get-tuple-element.47.shear, ...), custom_call_target="tpu_custom_call" | custom-call | tf_op jit(solution)/shard_map/first/pallas_call | solution.py:721
  19.7 0.0 collective-permute-start
  19.7 5.2 %collective-permute-start.1 = (f32[96,128]{1,0:T(8,128)}, f32[96,128]{1,0:T(8,128)}, u32[]{:S(2)}, u32[]{:S(2)}) collective-permute-start(f32[96,128]{1,0:T(8,128)} %get-tuple-element.51), channel_id=1, source_target_pairs={{0,120},{8,16},{16,8},{24,32},{32,24},{40,48},{48,40},{56,64},{64,... | collective-permute-start | bytes 147464 | tf_op jit(solution)/shard_map/ppermute | solution.py:630
  24.8 0.0 collective-permute-done.even_in
  24.8 2.1 %collective-permute-done.1.odd_in = f32[96,128]{1,0:T(8,128)} collective-permute-done((f32[96,128]{1,0:T(8,128)}, f32[96,128]{1,0:T(8,128)}, u32[]{:S(2)}, u32[]{:S(2)}) %collective-permute-start.1) | collective-permute-done | bytes 49184 | tf_op jit(solution)/shard_map/ppermute | solution.py:630
  26.9 1.0 middle.4
  27.9 3.0 %collective-permute-start.2 = (f32[64,128]{1,0:T(8,128)S(1)}, f32[64,128]{1,0:T(8,128)S(1)}, u32[]{:S(2)}, u32[]{:S(2)}) collective-permute-start(f32[64,128]{1,0:T(8,128)S(1)} %get-tuple-element.53), channel_id=1, source_target_pairs={{0,1},{1,0},{2,3},{3,2},{4,5},{5,4},{6,7},{7,6},{8,9},{9,8},{10,11... | collective-permute-start | bytes 98312 | tf_op jit(solution)/shard_map/ppermute | solution.py:631
  30.9 2.8 %collective-permute-start.3 = (f32[64,128]{1,0:T(8,128)S(1)}, f32[64,128]{1,0:T(8,128)S(1)}, u32[]{:S(2)}, u32[]{:S(2)}) collective-permute-start(f32[64,128]{1,0:T(8,128)S(1)} %get-tuple-element.54), channel_id=1, source_target_pairs={{1,2},{2,1},{3,4},{4,3},{5,6},{6,5},{9,10},{10,9},{11,12},{12,11},... | collective-permute-start | bytes 98312 | tf_op jit(solution)/shard_map/ppermute | solution.py:630
  33.7 0.0 collective-permute-done.2.even_in
  33.7 5.4 %collective-permute-done.3.odd_in = f32[64,128]{1,0:T(8,128)S(1)} collective-permute-done((f32[64,128]{1,0:T(8,128)S(1)}, f32[64,128]{1,0:T(8,128)S(1)}, u32[]{:S(2)}, u32[]{:S(2)}) %collective-permute-start.3) | collective-permute-done | bytes 32800 | tf_op jit(solution)/shard_map/ppermute | solution.py:630
  39.1 1.8 %step.3 = (f32[768,128]{1,0:T(8,128)S(1)}, f32[768,128]{1,0:T(8,128)S(1)}, f32[768,128]{1,0:T(8,128)S(1)}, f32[10,128]{1,0:T(8,128)S(1)}, f32[96,128]{1,0:T(8,128)S(1)}, /*index=5*/f32[96,128]{1,0:T(8,128)S(1)}) custom-call(s32[1]{0:T(128)} %bitcast.2.blk, s32[1]{0:T(128)} %bitcast.1.lat, f32[768,128]{1,0:T(8,128)S(1)} %get-tuple-element.52.old, ...), custom_call_target="tpu_custom_call" | custom-call | tf_op jit(solution)/shard_map/step/pallas_call | solution.py:730
  40.9 0.1 collective-permute-start.4
  41.0 2.0 %collective-permute-start.5 = (f32[96,128]{1,0:T(8,128)S(1)}, f32[96,128]{1,0:T(8,128)S(1)}, u32[]{:S(2)}, u32[]{:S(2)}) collective-permute-start(f32[96,128]{1,0:T(8,128)S(1)} %get-tuple-element.59), channel_id=1, source_target_pairs={{0,120},{8,16},{16,8},{24,32},{32,24},{40,48},{48,40},{56,64},{64,... | collective-permute-start | bytes 147464 | tf_op jit(solution)/shard_map/ppermute | solution.py:630
  43.0 0.0 collective-permute-done.4.even_in
  43.0 4.2 %collective-permute-done.5.odd_in = f32[96,128]{1,0:T(8,128)S(1)} collective-permute-done((f32[96,128]{1,0:T(8,128)S(1)}, f32[96,128]{1,0:T(8,128)S(1)}, u32[]{:S(2)}, u32[]{:S(2)}) %collective-permute-start.5) | collective-permute-done | bytes 49184 | tf_op jit(solution)/shard_map/ppermute | solution.py:630
  47.1 0.2 middle.5
  47.3 0.1 collective-permute-start.6
  47.4 5.7 %collective-permute-start.7 = (f32[64,128]{1,0:T(8,128)S(1)}, f32[64,128]{1,0:T(8,128)S(1)}, u32[]{:S(2)}, u32[]{:S(2)}) collective-permute-start(f32[64,128]{1,0:T(8,128)S(1)} %get-tuple-element.62), channel_id=1, source_target_pairs={{1,2},{2,1},{3,4},{4,3},{5,6},{6,5},{9,10},{10,9},{11,12},{12,11},... | collective-permute-start | bytes 98312 | tf_op jit(solution)/shard_map/ppermute | solution.py:630
  53.1 0.0 collective-permute-done.6.even_in
  53.1 2.5 %collective-permute-done.7.odd_in = f32[64,128]{1,0:T(8,128)S(1)} collective-permute-done((f32[64,128]{1,0:T(8,128)S(1)}, f32[64,128]{1,0:T(8,128)S(1)}, u32[]{:S(2)}, u32[]{:S(2)}) %collective-permute-start.7) | collective-permute-done | bytes 32800 | tf_op jit(solution)/shard_map/ppermute | solution.py:630
  55.6 1.8 %step.4 = (f32[768,128]{1,0:T(8,128)S(1)}, f32[768,128]{1,0:T(8,128)S(1)}, f32[768,128]{1,0:T(8,128)S(1)}, f32[10,128]{1,0:T(8,128)S(1)}, f32[96,128]{1,0:T(8,128)S(1)}, /*index=5*/f32[96,128]{1,0:T(8,128)S(1)}) custom-call(s32[1]{0:T(128)} %bitcast.2.blk, s32[1]{0:T(128)} %bitcast.1.lat, f32[768,128]{1,0:T(8,128)S(1)} %get-tuple-element.60.old, ...), custom_call_target="tpu_custom_call" | custom-call | tf_op jit(solution)/shard_map/step/pallas_call | solution.py:730
  57.5 0.1 collective-permute-start.8
  57.6 0.4 collective-permute-start.9
  58.0 0.8 collective-permute-done.8.even_in
  58.8 4.5 %collective-permute-done.9.odd_in = f32[96,128]{1,0:T(8,128)S(1)} collective-permute-done((f32[96,128]{1,0:T(8,128)S(1)}, f32[96,128]{1,0:T(8,128)S(1)}, u32[]{:S(2)}, u32[]{:S(2)}) %collective-permute-start.9) | collective-permute-done | bytes 49184 | tf_op jit(solution)/shard_map/ppermute | solution.py:630
  63.3 0.2 middle.6
  63.4 0.1 collective-permute-start.10
  63.5 6.2 %collective-permute-start.11 = (f32[64,128]{1,0:T(8,128)S(1)}, f32[64,128]{1,0:T(8,128)S(1)}, u32[]{:S(2)}, u32[]{:S(2)}) collective-permute-start(f32[64,128]{1,0:T(8,128)S(1)} %get-tuple-element.70), channel_id=1, source_target_pairs={{1,2},{2,1},{3,4},{4,3},{5,6},{6,5},{9,10},{10,9},{11,12},{12,11},... | collective-permute-start | bytes 98312 | tf_op jit(solution)/shard_map/ppermute | solution.py:630
  69.7 0.0 collective-permute-done.10.even_in
  69.7 2.0 %collective-permute-done.11.odd_in = f32[64,128]{1,0:T(8,128)S(1)} collective-permute-done((f32[64,128]{1,0:T(8,128)S(1)}, f32[64,128]{1,0:T(8,128)S(1)}, u32[]{:S(2)}, u32[]{:S(2)}) %collective-permute-start.11) | collective-permute-done | bytes 32800 | tf_op jit(solution)/shard_map/ppermute | solution.py:630
  71.7 0.0 copy-start.3
  71.7 0.0 copy-start.2
  71.7 1.8 %step.5 = (f32[768,128]{1,0:T(8,128)S(1)}, f32[768,128]{1,0:T(8,128)S(1)}, f32[768,128]{1,0:T(8,128)S(1)}, f32[10,128]{1,0:T(8,128)S(1)}, f32[96,128]{1,0:T(8,128)S(1)}, /*index=5*/f32[96,128]{1,0:T(8,128)S(1)}) custom-call(s32[1]{0:T(128)} %bitcast.2.blk, s32[1]{0:T(128)} %bitcast.1.lat, f32[768,128]{1,0:T(8,128)S(1)} %get-tuple-element.68.old, ...), custom_call_target="tpu_custom_call" | custom-call | tf_op jit(solution)/shard_map/step/pallas_call | solution.py:730
  73.6 0.1 collective-permute-start.12
  73.7 0.1 collective-permute-start.13
  73.8 1.1 %collective-permute-done.12.even_in = f32[96,128]{1,0:T(8,128)S(1)} collective-permute-done((f32[96,128]{1,0:T(8,128)S(1)}, f32[96,128]{1,0:T(8,128)S(1)}, u32[]{:S(2)}, u32[]{:S(2)}) %collective-permute-start.12) | collective-permute-done | bytes 49184 | tf_op jit(solution)/shard_map/ppermute | solution.py:631
  74.9 4.8 %collective-permute-done.13.odd_in = f32[96,128]{1,0:T(8,128)S(1)} collective-permute-done((f32[96,128]{1,0:T(8,128)S(1)}, f32[96,128]{1,0:T(8,128)S(1)}, u32[]{:S(2)}, u32[]{:S(2)}) %collective-permute-start.13) | collective-permute-done | bytes 49184 | tf_op jit(solution)/shard_map/ppermute | solution.py:630
  79.7 0.2 middle.7
  79.9 0.1 collective-permute-start.14
  80.0 9.1 %collective-permute-start.15 = (f32[64,128]{1,0:T(8,128)S(1)}, f32[64,128]{1,0:T(8,128)S(1)}, u32[]{:S(2)}, u32[]{:S(2)}) collective-permute-start(f32[64,128]{1,0:T(8,128)S(1)} %get-tuple-element.78), channel_id=1, source_target_pairs={{1,2},{2,1},{3,4},{4,3},{5,6},{6,5},{9,10},{10,9},{11,12},{12,11},... | collective-permute-start | bytes 98312 | tf_op jit(solution)/shard_map/ppermute | solution.py:630
  89.0 0.0 copy-done.3
  89.0 0.9 spectrum.1
  90.0 0.0 collective-permute-done.14.even_in
  90.0 1.0 collective-permute-done.15.odd_in
  90.9 0.0 copy-done.2
  90.9 12.9 %last.1 = (f32[3,2,9945]{2,1,0:T(2,128)}, f32[3,2,9945]{2,1,0:T(2,128)}) custom-call(s32[125,1,128]{2,1,0:T(1,128)} %reshape.21.columns_hbm, s32[16000]{0:T(1024)S(1)} %bitcast.12, s32[1]{0:T(128)} %bitcast.1.lat, f32[768,128]{1,0:T(8,128)S(1)} %get-tuple-element.76.old, f32[64,128]{1,0:T(8,128)S(1)} %collective-permute-done.14.even_in, ...), custom_call_target="tpu_custom_call" | custom-call | tf_op jit(solution)/shard_map/last/pallas_call | solution.py:781
Async XLA Ops:
  0.6 16.7 %copy-start = (bf16[128,1152]{1,0:T(8,128)(2,1)S(1)}, bf16[128,1152]{1,0:T(8,128)(2,1)}, u32[]{:S(2)}) copy-start(bf16[128,1152]{1,0:T(8,128)(2,1)} %constant.20.clone.divergence) | copy-start | bytes 884740
  0.6 16.7 %copy-start.1 = (bf16[384,384]{1,0:T(8,128)(2,1)S(1)}, bf16[384,384]{1,0:T(8,128)(2,1)}, u32[]{:S(2)}) copy-start(bf16[384,384]{1,0:T(8,128)(2,1)} %constant.19.clone.gradient) | copy-start | bytes 884740
  19.7 5.2 %collective-permute-start = (f32[96,128]{1,0:T(8,128)}, f32[96,128]{1,0:T(8,128)}, u32[]{:S(2)}, u32[]{:S(2)}) collective-permute-start(f32[96,128]{1,0:T(8,128)} %get-tuple-element.50), channel_id=1, source_target_pairs={{0,8},{8,0},{16,24},{24,16},{32,40},{40,32},{48,56},{56,48},{64,72... | collective-permute-start | bytes 147464 | tf_op jit(solution)/shard_map/ppermute | solution.py:631
  19.7 7.2 %collective-permute-start.1 = (f32[96,128]{1,0:T(8,128)}, f32[96,128]{1,0:T(8,128)}, u32[]{:S(2)}, u32[]{:S(2)}) collective-permute-start(f32[96,128]{1,0:T(8,128)} %get-tuple-element.51), channel_id=1, source_target_pairs={{0,120},{8,16},{16,8},{24,32},{32,24},{40,48},{48,40},{56,64},{64,... | collective-permute-start | bytes 147464 | tf_op jit(solution)/shard_map/ppermute | solution.py:630
  27.9 5.8 %collective-permute-start.2 = (f32[64,128]{1,0:T(8,128)S(1)}, f32[64,128]{1,0:T(8,128)S(1)}, u32[]{:S(2)}, u32[]{:S(2)}) collective-permute-start(f32[64,128]{1,0:T(8,128)S(1)} %get-tuple-element.53), channel_id=1, source_target_pairs={{0,1},{1,0},{2,3},{3,2},{4,5},{5,4},{6,7},{7,6},{8,9},{9,8},{10,11... | collective-permute-start | bytes 98312 | tf_op jit(solution)/shard_map/ppermute | solution.py:631
  30.9 8.2 %collective-permute-start.3 = (f32[64,128]{1,0:T(8,128)S(1)}, f32[64,128]{1,0:T(8,128)S(1)}, u32[]{:S(2)}, u32[]{:S(2)}) collective-permute-start(f32[64,128]{1,0:T(8,128)S(1)} %get-tuple-element.54), channel_id=1, source_target_pairs={{1,2},{2,1},{3,4},{4,3},{5,6},{6,5},{9,10},{10,9},{11,12},{12,11},... | collective-permute-start | bytes 98312 | tf_op jit(solution)/shard_map/ppermute | solution.py:630
  40.9 2.1 %collective-permute-start.4 = (f32[96,128]{1,0:T(8,128)S(1)}, f32[96,128]{1,0:T(8,128)S(1)}, u32[]{:S(2)}, u32[]{:S(2)}) collective-permute-start(f32[96,128]{1,0:T(8,128)S(1)} %get-tuple-element.58), channel_id=1, source_target_pairs={{0,8},{8,0},{16,24},{24,16},{32,40},{40,32},{48,56},{56,48},{64,72... | collective-permute-start | bytes 147464 | tf_op jit(solution)/shard_map/ppermute | solution.py:631
  41.0 6.1 %collective-permute-start.5 = (f32[96,128]{1,0:T(8,128)S(1)}, f32[96,128]{1,0:T(8,128)S(1)}, u32[]{:S(2)}, u32[]{:S(2)}) collective-permute-start(f32[96,128]{1,0:T(8,128)S(1)} %get-tuple-element.59), channel_id=1, source_target_pairs={{0,120},{8,16},{16,8},{24,32},{32,24},{40,48},{48,40},{56,64},{64,... | collective-permute-start | bytes 147464 | tf_op jit(solution)/shard_map/ppermute | solution.py:630
  47.3 5.8 %collective-permute-start.6 = (f32[64,128]{1,0:T(8,128)S(1)}, f32[64,128]{1,0:T(8,128)S(1)}, u32[]{:S(2)}, u32[]{:S(2)}) collective-permute-start(f32[64,128]{1,0:T(8,128)S(1)} %get-tuple-element.61), channel_id=1, source_target_pairs={{0,1},{1,0},{2,3},{3,2},{4,5},{5,4},{6,7},{7,6},{8,9},{9,8},{10,11... | collective-permute-start | bytes 98312 | tf_op jit(solution)/shard_map/ppermute | solution.py:631
  47.4 8.2 %collective-permute-start.7 = (f32[64,128]{1,0:T(8,128)S(1)}, f32[64,128]{1,0:T(8,128)S(1)}, u32[]{:S(2)}, u32[]{:S(2)}) collective-permute-start(f32[64,128]{1,0:T(8,128)S(1)} %get-tuple-element.62), channel_id=1, source_target_pairs={{1,2},{2,1},{3,4},{4,3},{5,6},{6,5},{9,10},{10,9},{11,12},{12,11},... | collective-permute-start | bytes 98312 | tf_op jit(solution)/shard_map/ppermute | solution.py:630
  57.5 1.3 %collective-permute-start.8 = (f32[96,128]{1,0:T(8,128)S(1)}, f32[96,128]{1,0:T(8,128)S(1)}, u32[]{:S(2)}, u32[]{:S(2)}) collective-permute-start(f32[96,128]{1,0:T(8,128)S(1)} %get-tuple-element.66), channel_id=1, source_target_pairs={{0,8},{8,0},{16,24},{24,16},{32,40},{40,32},{48,56},{56,48},{64,72... | collective-permute-start | bytes 147464 | tf_op jit(solution)/shard_map/ppermute | solution.py:631
  57.6 5.7 %collective-permute-start.9 = (f32[96,128]{1,0:T(8,128)S(1)}, f32[96,128]{1,0:T(8,128)S(1)}, u32[]{:S(2)}, u32[]{:S(2)}) collective-permute-start(f32[96,128]{1,0:T(8,128)S(1)} %get-tuple-element.67), channel_id=1, source_target_pairs={{0,120},{8,16},{16,8},{24,32},{32,24},{40,48},{48,40},{56,64},{64,... | collective-permute-start | bytes 147464 | tf_op jit(solution)/shard_map/ppermute | solution.py:630
  63.4 6.3 %collective-permute-start.10 = (f32[64,128]{1,0:T(8,128)S(1)}, f32[64,128]{1,0:T(8,128)S(1)}, u32[]{:S(2)}, u32[]{:S(2)}) collective-permute-start(f32[64,128]{1,0:T(8,128)S(1)} %get-tuple-element.69), channel_id=1, source_target_pairs={{0,1},{1,0},{2,3},{3,2},{4,5},{5,4},{6,7},{7,6},{8,9},{9,8},{10,11... | collective-permute-start | bytes 98312 | tf_op jit(solution)/shard_map/ppermute | solution.py:631
  63.5 8.2 %collective-permute-start.11 = (f32[64,128]{1,0:T(8,128)S(1)}, f32[64,128]{1,0:T(8,128)S(1)}, u32[]{:S(2)}, u32[]{:S(2)}) collective-permute-start(f32[64,128]{1,0:T(8,128)S(1)} %get-tuple-element.70), channel_id=1, source_target_pairs={{1,2},{2,1},{3,4},{4,3},{5,6},{6,5},{9,10},{10,9},{11,12},{12,11},... | collective-permute-start | bytes 98312 | tf_op jit(solution)/shard_map/ppermute | solution.py:630
  71.7 17.3 %copy-start.3 = (bf16[640,128]{1,0:T(8,128)(2,1)S(1)}, bf16[640,128]{1,0:T(8,128)(2,1)}, u32[]{:S(2)}) copy-start(bf16[640,128]{1,0:T(8,128)(2,1)} %constant.23.clone.wide) | copy-start | bytes 491524
  71.7 19.2 %copy-start.2 = (s32[125,128]{1,0:T(8,128)S(1)}, s32[125,128]{1,0:T(8,128)}, u32[]{:S(2)}) copy-start(s32[125,128]{1,0:T(8,128)} %param.19) | copy-start | bytes 192004
  73.6 1.3 %collective-permute-start.12 = (f32[96,128]{1,0:T(8,128)S(1)}, f32[96,128]{1,0:T(8,128)S(1)}, u32[]{:S(2)}, u32[]{:S(2)}) collective-permute-start(f32[96,128]{1,0:T(8,128)S(1)} %get-tuple-element.74), channel_id=1, source_target_pairs={{0,8},{8,0},{16,24},{24,16},{32,40},{40,32},{48,56},{56,48},{64,72... | collective-permute-start | bytes 147464 | tf_op jit(solution)/shard_map/ppermute | solution.py:631
  73.7 6.0 %collective-permute-start.13 = (f32[96,128]{1,0:T(8,128)S(1)}, f32[96,128]{1,0:T(8,128)S(1)}, u32[]{:S(2)}, u32[]{:S(2)}) collective-permute-start(f32[96,128]{1,0:T(8,128)S(1)} %get-tuple-element.75), channel_id=1, source_target_pairs={{0,120},{8,16},{16,8},{24,32},{32,24},{40,48},{48,40},{56,64},{64,... | collective-permute-start | bytes 147464 | tf_op jit(solution)/shard_map/ppermute | solution.py:630
  79.9 10.1 %collective-permute-start.14 = (f32[64,128]{1,0:T(8,128)S(1)}, f32[64,128]{1,0:T(8,128)S(1)}, u32[]{:S(2)}, u32[]{:S(2)}) collective-permute-start(f32[64,128]{1,0:T(8,128)S(1)} %get-tuple-element.77), channel_id=1, source_target_pairs={{0,1},{1,0},{2,3},{3,2},{4,5},{5,4},{6,7},{7,6},{8,9},{9,8},{10,11... | collective-permute-start | bytes 98312 | tf_op jit(solution)/shard_map/ppermute | solution.py:631
  80.0 11.0 %collective-permute-start.15 = (f32[64,128]{1,0:T(8,128)S(1)}, f32[64,128]{1,0:T(8,128)S(1)}, u32[]{:S(2)}, u32[]{:S(2)}) collective-permute-start(f32[64,128]{1,0:T(8,128)S(1)} %get-tuple-element.78), channel_id=1, source_target_pairs={{1,2},{2,1},{3,4},{4,3},{5,6},{6,5},{9,10},{10,9},{11,12},{12,11},... | collective-permute-start | bytes 98312 | tf_op jit(solution)/shard_map/ppermute | solution.py:630
where the time goes:
time: 105 us; the launch traced here: 104 us
  Pallas kernels  38.2 us (36%)
  starting transfers between devices  34.8 us (33%)
  waiting for transfers between devices  28.3 us (27%)
  local copies, waits for them, and re-layouts  1.58 us (2%)
    ppermute x8, starting transfers between devices, exchange(): odd = lax.ppermute(odd, axis, odd_pairs)  31.3 us
    ppermute x8, waiting for transfers between devices, exchange(): odd = lax.ppermute(odd, axis, odd_pairs)  26.4 us
    pallas_call x1, Pallas kernels, local(): pl.pallas_call(gather_kernel, out_shape=(kept(24 * 128, 128), kept(768, 1...  15.1 us
    pallas_call x1, Pallas kernels, local(): pl.pallas_call(last_kernel, out_shape=(nodal, nodal), in_specs=[pl.BlockS...  12.9 us
    pallas_call x3, Pallas kernels, local(): pl.pallas_call(make_step_kernel(step), out_shape=(balance_shape, balance_...  5.49 us
    ppermute x8, starting transfers between devices, exchange(): even = lax.ppermute(even, axis, even_pairs)  3.5 us
    pallas_call x1, Pallas kernels, local(): pl.pallas_call(first_kernel, out_shape=(balance_shape, integral_shape, cy...  2.35 us
  transfers between devices with their start and end apart: 16, of which 10 were waited for; matrix products, arithmetic and copies ran while one was open for 0% of the time, Pallas kernels for 1%

commit v1 on v0

--- a/solution.py
+++ b/solution.py
@@ -101,66 +101,80 @@
     return pl.BlockSpec(memory_space=pltpu.VMEM)
 
 
+def hbm():
+    return pl.BlockSpec(memory_space=pltpu.HBM)
+
+
 def smem():
     return pl.BlockSpec(memory_space=pltpu.SMEM)
 
 
-def for_nodes(numbers, columns_hbm, chunks, sems, pair_places, visit):
-    def fetch(pair, slot):
-        row = 25 * lax.shift_right_logical(pair, 2) + 5 * (pair & 3)
+def start_pairs(numbers_hbm, chunks, sems, rounds, slots, pair_of):
+    def fetch(index, slot):
+        a, b = pair_of(index, slot)
+        start = pl.multiple_of(128 * (25 * a + 5 * b), 128)
         return pltpu.make_async_copy(
-            columns_hbm.at[pl.ds(row, 4)], chunks.at[slot], sems.at[slot]
-        )
-
-    for slot in range(SLOTS):
-        fetch(jnp.int32(slot), slot).start()
-
-    def some_pairs(index, carry):
-        for slot in range(SLOTS):
-            pair = SLOTS * index + slot
-            fetch(pair, slot).wait()
-            a, b = lax.shift_right_logical(pair, 2), pair & 3
-            for c in range(4):
-                places = pair_places(a, b, c)
-                for ex in range(EXB):
-                    for ey in range(EYL):
-                        for ez in range(EZ):
-                            node = chunks[slot, c, 0, 64 * ex + 16 * ey + ez]
-                            visit(places, c, ex, ey, ez, node)
-
-            @pl.when(index < 16 // SLOTS - 1)
-            def _():
-                fetch(pair + SLOTS, slot).start()
-
+            numbers_hbm.at[pl.ds(start, 512)], chunks.at[slot], sems.at[slot]
+        )
+
+    for slot in range(slots):
+        fetch(jnp.int32(0), slot).start()
+
+    def visit_pairs(pair_places, visit):
+        def one_round(index, carry):
+            for slot in range(slots):
+                a, b = pair_of(index, slot)
+                fetch(index, slot).wait()
+                for c in range(4):
+                    places = pair_places(a, b, c)
+                    for ex in range(EXB):
+                        for ey in range(EYL):
+                            for ez in range(EZ):
+                                node = chunks[slot, 128 * c + 64 * ex + 16 * ey + ez]
+                                visit(places, c, ex, ey, ez, node)
+                if rounds > 1:
+
+                    @pl.when(index < rounds - 1)
+                    def _():
+                        fetch(index + 1, slot).start()
+
+            return carry
+
+        lax.fori_loop(0, rounds, one_round, 0)
+
+    return visit_pairs
+
+
+def visit_line(numbers, ix, iy, points, pair_places, visit):
+    ex = jnp.minimum(lax.shift_right_logical(ix, 2), EXB - 1)
+    ey = jnp.minimum(lax.shift_right_logical(iy, 2), EYL - 1)
+    a, b = ix - 4 * ex, iy - 4 * ey
+    start = 3200 * a + 640 * b + 64 * ex + 16 * ey
+    for c in points:
+        places = pair_places(a, b, c)
+        for ez in range(EZ - 1 if c == 4 else 0, EZ):
+            visit(places, c, ex, ey, ez, numbers[start + 128 * c + ez])
+
+
+def visit_far(numbers, plane_rows, last_row, top_rows, pair_places, visit):
+    first, count = plane_rows
+
+    def plane_line(index, carry):
+        visit_line(numbers, jnp.int32(NXN - 1), index + first, range(4), pair_places, visit)
         return carry
 
-    lax.fori_loop(0, 16 // SLOTS, some_pairs, 0)
-
-    def far_line(ix, iy, c_count):
-        ex = jnp.minimum(lax.shift_right_logical(ix, 2), EXB - 1)
-        ey = jnp.minimum(lax.shift_right_logical(iy, 2), EYL - 1)
-        a, b = ix - 4 * ex, iy - 4 * ey
-        start = 3200 * a + 640 * b + 64 * ex + 16 * ey
-        for c in range(5 - c_count, 5) if c_count == 1 else range(c_count):
-            places = pair_places(a, b, c)
-            for ez in range(EZ - 1 if c == 4 else 0, EZ):
-                visit(places, c, ex, ey, ez, numbers[start + 128 * c + ez])
-
-    def last_plane(iy, carry):
-        far_line(jnp.int32(NXN - 1), iy, 4)
-        return carry
-
-    lax.fori_loop(0, NYN, last_plane, 0)
-
-    def last_row(ix, carry):
-        far_line(ix, jnp.int32(NYN - 1), 4)
-        return carry
-
-    lax.fori_loop(0, NXN - 1, last_row, 0)
+    lax.fori_loop(0, count, plane_line, 0)
+    if last_row:
+
+        def row_line(ix, carry):
+            visit_line(numbers, ix, jnp.int32(NYN - 1), range(4), pair_places, visit)
+            return carry
+
+        lax.fori_loop(0, NXN, row_line, 0)
 
     def top(ix, carry):
-        for iy in range(NYN):
-            far_line(ix, jnp.int32(iy), 1)
+        for iy in top_rows:
+            visit_line(numbers, ix, jnp.int32(iy), (4,), pair_places, visit)
         return carry
 
     lax.fori_loop(0, NXN, top, 0)
@@ -176,7 +190,6 @@
 
 
 def gather_kernel(
-    columns_hbm,
     numbers_hbm,
     sources_hbm,
     displacement_hbm,
@@ -187,12 +200,21 @@
     weight_hbm,
     pulses_hbm,
     frequency_hbm,
+    gradient_hbm,
+    divergence_hbm,
+    blk,
     force_out,
     motion_out,
     speed_out,
     inverse_out,
     shear_out,
     lame_out,
+    gradient,
+    divergence,
+    balance,
+    integral,
+    even_out,
+    odd_out,
     mixing,
     rows,
     table,
@@ -225,11 +247,16 @@
                 (shear_hbm, shear),
                 (lame_hbm, lame),
                 (weight_hbm, weight),
+                (gradient_hbm, gradient),
+                (divergence_hbm, divergence),
             )
         )
     ]
     for copy in copies:
         copy.start()
+    visit_pairs = start_pairs(
+        numbers_hbm, chunks, chunk_sems, 4, 4, lambda index, slot: (index, slot)
+    )
     for copy in copies[0:2]:
         copy.wait()
     index = lax.broadcasted_iota(jnp.int32, (NFREQ, EVENTS), 0)
@@ -273,7 +300,8 @@
         at = place + ((4 * ex * NYN + 4 * ey) * LINE + 4 * ez)
         lines[pl.ds(at, 1), :] = table[pl.ds(node, 1), :]
 
-    for_nodes(numbers, columns_hbm, chunks, chunk_sems, line_places, gather_node)
+    visit_pairs(line_places, gather_node)
+    visit_far(numbers, (0, NYN - 1), True, range(NYN), line_places, gather_node)
 
     lanes = lanes_of(128)
 
@@ -312,6 +340,8 @@
     shear_out[125:128, :] = jnp.zeros((3, 128), f32)
     lame_out[0:125, :] = lame[...] * weight[0:125, :]
     lame_out[125:128, :] = jnp.zeros((3, 128), f32)
+    balance_of(motion_out, force_out, 0, shear_out, lame_out, gradient, divergence, balance, integral)
+    pack_cycle(balance, blk, even_out, odd_out)
 
 
 def lanes_of(count):
@@ -478,13 +508,6 @@
                 base = 128 * j + 25 * a
                 balance[base : base + 5, :] += jnp.where(slot == 0, turn(low, -t), 0.0)
                 balance[base + 20 : base + 25, :] += jnp.where(slot == 3, turn(up, 3 - t), 0.0)
-
-
-def first_kernel(
-    blk, motion, force, shear, lame, gradient, divergence, balance, integral, even_out, odd_out
-):
-    balance_of(motion, force, 0, shear, lame, gradient, divergence, balance, integral)
-    pack_cycle(balance, blk, even_out, odd_out)
 
 
 def middle_kernel(blk, lat, old, even_in, odd_in, balance, even_out, odd_out):
@@ -533,9 +556,78 @@
     return step_kernel
 
 
+def scatter_to(table, state, points):
+    def point_rows(group):
+        values = jnp.concatenate(
+            [state[pl.ds(group * 8 + part, 16, stride=128), :] for part in range(8)], axis=0
+        )
+        start = pl.multiple_of(group * 128, 128)
+        points[pl.ds(start, 128), :] = values.T
+
+    for_blocks(16, 4, point_rows)
+    part_of = lanes_of(1) // 16
+
+    def point_places(a, b, c):
+        point = 25 * a + 5 * b + c
+        return lax.shift_right_logical(point, 3) * 128, part_of == (point & 7)
+
+    def scatter_node(places, c, ex, ey, ez, node):
+        del c
+        at = places[0] + (64 * ex + 16 * ey + ez)
+        table[pl.ds(node, 1), :] = jnp.where(places[1], points[pl.ds(at, 1), :], 0.0)
+
+    return point_places, scatter_node
+
+
+def state_of(balance, inverse, motion_in, speed_in, state):
+    scale = inverse[...]
+    for j in range(6):
+        part = slice(128 * j, 128 * j + 128)
+        now = speed_in[part, :] + balance[part, :] * scale
+        state[768 + 128 * j : 896 + 128 * j, :] = now
+        state[part, :] = motion_in[part, :] + now
+
+
+def inner_kernel(
+    numbers_hbm, balance, inverse, motion_in, speed_in, table, state, points, chunks, sems
+):
+    visit_pairs = start_pairs(
+        numbers_hbm, chunks, sems, 3, 3, lambda index, slot: (index + 1, slot + 1)
+    )
+    state_of(balance, inverse, motion_in, speed_in, state)
+    visit_pairs(*scatter_to(table, state, points))
+
+
+def outer_kernel(
+    numbers_hbm,
+    balance,
+    inverse,
+    motion_in,
+    speed_in,
+    table_in,
+    table,
+    state,
+    points,
+    chunks,
+    sems,
+    numbers,
+    whole_sem,
+):
+    del table_in
+    whole = pltpu.make_async_copy(numbers_hbm, numbers, whole_sem)
+    whole.start()
+    visit_pairs = start_pairs(
+        numbers_hbm, chunks, sems, 1, 3, lambda index, slot: (index, slot + 1)
+    )
+    state_of(balance, inverse, motion_in, speed_in, state)
+    places, visit = scatter_to(table, state, points)
+    visit_pairs(places, visit)
+    whole.wait()
+    visit_far(numbers, (1, NYN - 2), False, range(1, NYN - 1), places, visit)
+
+
 def last_kernel(
-    columns_hbm,
-    numbers,
+    numbers_hbm,
     lat,
     old,
     even_in,
@@ -543,48 +635,29 @@
     inverse,
     motion_in,
     speed_in,
+    table_in,
     motion_out,
     speed_out,
+    table,
     balance,
     state,
     points,
-    table,
     chunks,
-    chunk_sems,
+    sems,
+    numbers,
+    whole_sem,
 ):
-    advance(
-        lat,
-        old,
-        even_in,
-        odd_in,
-        inverse,
-        motion_in,
-        speed_in,
-        state.at[0:768, :],
-        state.at[768:1536, :],
-        balance,
-    )
-
-    def point_rows(group):
-        values = jnp.concatenate(
-            [state[pl.ds(group * 8 + part, 16, stride=128), :] for part in range(8)], axis=0
-        )
-        start = pl.multiple_of(group * 128, 128)
-        points[pl.ds(start, 128), :] = values.T
-
-    for_blocks(16, 4, point_rows)
-    part_of = lanes_of(1) // 16
-
-    def point_places(a, b, c):
-        point = 25 * a + 5 * b + c
-        return lax.shift_right_logical(point, 3) * 128, part_of == (point & 7)
-
-    def scatter_node(places, c, ex, ey, ez, node):
-        del c
-        at = places[0] + (64 * ex + 16 * ey + ez)
-        table[pl.ds(node, 1), :] = jnp.where(places[1], points[pl.ds(at, 1), :], 0.0)
-
-    for_nodes(numbers, columns_hbm, chunks, chunk_sems, point_places, scatter_node)
+    del table_in
+    whole = pltpu.make_async_copy(numbers_hbm, numbers, whole_sem)
+    whole.start()
+    visit_pairs = start_pairs(numbers_hbm, chunks, sems, 1, 4, lambda index, slot: (slot, index))
+    balance[...] = old[...]
+    add_lat(balance, lat, even_in, odd_in)
+    state_of(balance, inverse, motion_in, speed_in, state)
+    places, visit = scatter_to(table, state, points)
+    visit_pairs(places, visit)
+    whole.wait()
+    visit_far(numbers, (0, 1), True, (0, NYN - 1), places, visit)
 
     def turned(start):
         values = table[pl.ds(start, 128), :].T
@@ -651,7 +724,6 @@
     blk = lax.axis_index("blk").astype(jnp.int32).reshape(1)
     lat = lax.axis_index("lat").astype(jnp.int32).reshape(1)
     numbers = node_numbers.reshape(125 * 128)
-    columns = node_numbers.reshape(125, 1, 128)
     blk_count = lax.axis_size("blk")
     lat_count = lax.axis_size("lat")
     cycle_even = [(i, i ^ 1) for i in range(blk_count)]
@@ -659,7 +731,22 @@
     lat_even = [(i, i ^ 1) for i in range(lat_count)]
     lat_odd = [(i, ((i + 1) ^ 1) - 1) for i in range(1, lat_count - 1)]
 
-    force, motion, speed, inverse, shear, lame = pl.pallas_call(
+    balance_shape, integral_shape = kept(768, 128), kept(10, 128)
+    cycle_shape, lat_shape = kept(96, 128), kept(64, 128)
+    (
+        force,
+        motion,
+        speed,
+        inverse,
+        shear,
+        lame,
+        gradient,
+        divergence,
+        balance,
+        integral,
+        even,
+        odd,
+    ) = pl.pallas_call(
         gather_kernel,
         out_shape=(
             kept(24 * 128, 128),
@@ -668,9 +755,15 @@
             kept(128, 128),
             kept(128, 128),
             kept(128, 128),
+            pltpu.VMEM((384, 384), bf16),
+            pltpu.VMEM((128, 1152), bf16),
+            balance_shape,
+            integral_shape,
+            cycle_shape,
+            cycle_shape,
         ),
-        in_specs=[pl.BlockSpec(memory_space=pltpu.HBM)] * 11,
-        out_specs=[vmem()] * 6,
+        in_specs=[hbm()] * 12 + [smem()],
+        out_specs=[vmem()] * 12,
         scratch_shapes=[
             pltpu.VMEM((24, 3 * EVENTS), f32),
             pltpu.VMEM((COMPS, NODE_BLOCKS * 128), f32),
@@ -686,8 +779,8 @@
             pltpu.VMEM((128, 128), f32),
             pltpu.VMEM((8, NFREQ), bf16),
             pltpu.VMEM((2, EVENTS), jnp.int32),
-            pltpu.SemaphoreType.DMA((10,)),
-            pltpu.SMEM((SLOTS, 4, 1, 128), jnp.int32),
+            pltpu.SemaphoreType.DMA((12,)),
+            pltpu.SMEM((SLOTS, 512), jnp.int32),
             pltpu.SemaphoreType.DMA((SLOTS,)),
         ],
         compiler_params=limit(24),
@@ -696,7 +789,6 @@
         *(
             pltpu.with_memory_space_constraint(array, pltpu.HBM)
             for array in (
-                columns,
                 numbers,
                 adjoint_sources.transpose(1, 0, 2),
                 displacement.transpose(1, 0, 2),
@@ -707,26 +799,27 @@
                 weight,
                 jnp.asarray(pulses),
                 event_frequency,
+                gradient,
+                divergence,
             )
-        )
+        ),
+        blk,
     )
     force, motion, speed, inverse, shear, lame, gradient, divergence = hold(
         force, motion, speed, inverse, shear, lame, gradient, divergence
     )
-    balance_shape, integral_shape = kept(768, 128), kept(10, 128)
-    cycle_shape, lat_shape = kept(96, 128), kept(64, 128)
     integrals = []
+    numbers_hbm = pltpu.with_memory_space_constraint(numbers, pltpu.HBM)
+    table_shape = kept(NODE_BLOCKS * 128, 128)
+    scatter_scratch = [
+        pltpu.VMEM((2048, 128), f32),
+        pltpu.VMEM((16 * 128, 128), f32),
+        pltpu.SMEM((SLOTS, 512), jnp.int32),
+        pltpu.SemaphoreType.DMA((SLOTS,)),
+    ]
+    whole_scratch = [pltpu.SMEM((125 * 128,), jnp.int32), pltpu.SemaphoreType.DMA]
     for step in range(STEP_TOTAL):
-        if step == 0:
-            balance, integral, even, odd = pl.pallas_call(
-                first_kernel,
-                out_shape=(balance_shape, integral_shape, cycle_shape, cycle_shape),
-                in_specs=[smem()] + [vmem()] * 6,
-                out_specs=[vmem()] * 4,
-                compiler_params=limit(8),
-                name="first",
-            )(blk, motion, force, shear, lame, gradient, divergence)
-        else:
+        if step > 0:
             balance, motion, speed, integral, even, odd = pl.pallas_call(
                 make_step_kernel(step),
                 out_shape=(
@@ -759,6 +852,16 @@
             motion, speed = hold(motion, speed)
         integrals.append(integral)
         odd, even = exchange("blk", odd, even, cycle_odd, cycle_even)
+        if step == STEP_TOTAL - 1:
+            table = pl.pallas_call(
+                inner_kernel,
+                out_shape=table_shape,
+                in_specs=[hbm()] + [vmem()] * 4,
+                out_specs=vmem(),
+                scratch_shapes=scatter_scratch,
+                compiler_params=limit(16),
+                name="inner",
+            )(numbers_hbm, *hold(balance, inverse, motion, speed))
         balance, even, odd = pl.pallas_call(
             middle_kernel,
             out_shape=(balance_shape, lat_shape, lat_shape),
@@ -769,6 +872,16 @@
         )(blk, lat, *hold(balance, even, odd))
         odd, even = exchange("lat", odd, even, lat_odd, lat_even)
         balance, even, odd = hold(balance, even, odd)
+    table = pl.pallas_call(
+        outer_kernel,
+        out_shape=table_shape,
+        in_specs=[hbm()] + [vmem()] * 5,
+        out_specs=vmem(),
+        scratch_shapes=scatter_scratch + whole_scratch,
+        input_output_aliases={5: 0},
+        compiler_params=limit(16),
+        name="outer",
+    )(numbers_hbm, *hold(balance, inverse, motion, speed, table))
     spectrum = pl.pallas_call(
         spectrum_kernel,
         out_shape=jax.ShapeDtypeStruct((640, 128), f32),
@@ -778,31 +891,19 @@
         name="spectrum",
     )(*hold(jnp.asarray(wide), *integrals))
     nodal = jax.ShapeDtypeStruct((3, 2, NODES_DEV), f32)
-    final_motion, final_speed = pl.pallas_call(
+    final_motion, final_speed, _ = pl.pallas_call(
         last_kernel,
-        out_shape=(nodal, nodal),
-        in_specs=[pl.BlockSpec(memory_space=pltpu.HBM)] + [smem()] * 2 + [vmem()] * 6,
-        out_specs=[vmem()] * 2,
-        scratch_shapes=[
-            pltpu.VMEM((768, 128), f32),
-            pltpu.VMEM((2048, 128), f32),
-            pltpu.VMEM((16 * 128, 128), f32),
-            pltpu.VMEM((NODE_BLOCKS * 128, 128), f32),
-            pltpu.SMEM((SLOTS, 4, 1, 128), jnp.int32),
-            pltpu.SemaphoreType.DMA((SLOTS,)),
-        ],
-        compiler_params=limit(24),
+        out_shape=(nodal, nodal, table_shape),
+        in_specs=[hbm(), smem()] + [vmem()] * 7,
+        out_specs=[vmem()] * 3,
+        scratch_shapes=[pltpu.VMEM((768, 128), f32)] + scatter_scratch + whole_scratch,
+        input_output_aliases={8: 2},
+        compiler_params=limit(16),
         name="last",
     )(
-        pltpu.with_memory_space_constraint(columns, pltpu.HBM),
-        numbers,
+        numbers_hbm,
         lat,
-        balance,
-        even,
-        odd,
-        inverse,
-        motion,
-        speed,
+        *hold(balance, even, odd, inverse, motion, speed, table),
     )
     return (
         final_motion.transpose(1, 0, 2),

time: 105 us -> 102 us (0.971)
  local copies, waits for them, and re-layouts: 1.58 us -> 0.01 us
    pallas_call x2 -> x3, Pallas kernels: 15.2 us -> 13.3 us  [the longest x1 6.12 us: local(): pl.pallas_call(last_kernel, out_shape=(nodal, nodal, table_shape), in_spe...]
    pallas_call x1, Pallas kernels: 15.1 us -> 16.8 us  [local(): pl.pallas_call(gather_kernel, out_shape=(kept(24 * 128, 128), kept(768, 1...]
    reshape x1 -> x0, local copies, waits for them, and re-layouts: 1.56 us -> none  [local(): columns = node_numbers.reshape(125, 1, 128)]
  transfers between devices with their start and end apart: 16 -> 16, of which waited for: 10 -> 9; matrix products, arithmetic and copies ran while one was open for 0% -> 0% of each run, Pallas kernels for 1% -> 8%
where the time goes in v1:
time: 102 us; the launch traced here: 101 us
  Pallas kernels  38 us (37%)
  starting transfers between devices  34.9 us (34%)
  waiting for transfers between devices  27.5 us (27%)
  between operations  1.02 us (1%)
    ppermute x8, starting transfers between devices, exchange(): odd = lax.ppermute(odd, axis, odd_pairs)  31.3 us
    ppermute x8, waiting for transfers between devices, exchange(): odd = lax.ppermute(odd, axis, odd_pairs)  25.5 us
    pallas_call x1, Pallas kernels, local(): pl.pallas_call(gather_kernel, out_shape=(kept(24 * 128, 128), kept(768, 1...  16.8 us
    pallas_call x1, Pallas kernels, local(): pl.pallas_call(last_kernel, out_shape=(nodal, nodal, table_shape), in_spe...  6.12 us
    pallas_call x3, Pallas kernels, local(): pl.pallas_call(make_step_kernel(step), out_shape=(balance_shape, balance_...  5.48 us
    pallas_call x1, Pallas kernels, local(): pl.pallas_call(inner_kernel, out_shape=table_shape, in_specs=[hbm()] + [v...  3.74 us
    ppermute x8, starting transfers between devices, exchange(): even = lax.ppermute(even, axis, even_pairs)  3.58 us
    pallas_call x1, Pallas kernels, local(): pl.pallas_call(outer_kernel, out_shape=table_shape, in_specs=[hbm()] + [v...  3.46 us
  transfers between devices with their start and end apart: 16, of which 9 were waited for; matrix products, arithmetic and copies ran while one was open for 0% of the time, Pallas kernels for 8%

profile of v1, /device:TPU:6, one launch (start us, length us, event | category | flops | bytes accessed | tf_op | source)
XLA Modules:
  0.0 101.4 jit_solution(7754927259635412530)
XLA Ops:
  0.6 16.8 %gather.1 = (f32[3072,128]{1,0:T(8,128)S(1)}, f32[768,128]{1,0:T(8,128)S(1)}, f32[768,128]{1,0:T(8,128)S(1)}, f32[128,128]{1,0:T(8,128)S(1)}, f32[128,128]{1,0:T...) custom-call(s32[16000]{0:T(1024)} %bitcast.12, ...), custom_call_target="tpu_custom_call" | custom-call | tf_op jit(solution)/shard_map/gather/pallas_call | solution.py:749
  17.4 0.1 collective-permute-start
  17.5 5.1 %collective-permute-start.1 = (f32[96,128]{1,0:T(8,128)}, f32[96,128]{1,0:T(8,128)}, u32[]{:S(2)}, u32[]{:S(2)}) collective-permute-start(f32[96,128]{1,0:T(8,128)} %get-tuple-element.49), channel_id=1, source_target_pairs={{0,120},{8,16},{16,8},{24,32},{32,24},{40,48},{48,40},{56,64},{64,... | collective-permute-start | bytes 147464 | tf_op jit(solution)/shard_map/ppermute | solution.py:703
  22.7 0.0 collective-permute-done.even_in
  22.7 2.1 %collective-permute-done.1.odd_in = f32[96,128]{1,0:T(8,128)} collective-permute-done((f32[96,128]{1,0:T(8,128)}, f32[96,128]{1,0:T(8,128)}, u32[]{:S(2)}, u32[]{:S(2)}) %collective-permute-start.1) | collective-permute-done | bytes 49184 | tf_op jit(solution)/shard_map/ppermute | solution.py:703
  24.7 1.0 middle.4
  25.8 3.0 %collective-permute-start.2 = (f32[64,128]{1,0:T(8,128)S(1)}, f32[64,128]{1,0:T(8,128)S(1)}, u32[]{:S(2)}, u32[]{:S(2)}) collective-permute-start(f32[64,128]{1,0:T(8,128)S(1)} %get-tuple-element.51), channel_id=1, source_target_pairs={{0,1},{1,0},{2,3},{3,2},{4,5},{5,4},{6,7},{7,6},{8,9},{9,8},{10,11... | collective-permute-start | bytes 98312 | tf_op jit(solution)/shard_map/ppermute | solution.py:704
  28.7 2.8 %collective-permute-start.3 = (f32[64,128]{1,0:T(8,128)S(1)}, f32[64,128]{1,0:T(8,128)S(1)}, u32[]{:S(2)}, u32[]{:S(2)}) collective-permute-start(f32[64,128]{1,0:T(8,128)S(1)} %get-tuple-element.52), channel_id=1, source_target_pairs={{1,2},{2,1},{3,4},{4,3},{5,6},{6,5},{9,10},{10,9},{11,12},{12,11},... | collective-permute-start | bytes 98312 | tf_op jit(solution)/shard_map/ppermute | solution.py:703
  31.5 0.0 collective-permute-done.2.even_in
  31.5 5.4 %collective-permute-done.3.odd_in = f32[64,128]{1,0:T(8,128)S(1)} collective-permute-done((f32[64,128]{1,0:T(8,128)S(1)}, f32[64,128]{1,0:T(8,128)S(1)}, u32[]{:S(2)}, u32[]{:S(2)}) %collective-permute-start.3) | collective-permute-done | bytes 32800 | tf_op jit(solution)/shard_map/ppermute | solution.py:703
  36.9 1.8 %step.3 = (f32[768,128]{1,0:T(8,128)S(1)}, f32[768,128]{1,0:T(8,128)S(1)}, f32[768,128]{1,0:T(8,128)S(1)}, f32[10,128]{1,0:T(8,128)S(1)}, f32[96,128]{1,0:T(8,128)S(1)}, /*index=5*/f32[96,128]{1,0:T(8,128)S(1)}) custom-call(s32[1]{0:T(128)} %bitcast.2.blk, s32[1]{0:T(128)} %bitcast.1.lat, f32[768,128]{1,0:T(8,128)S(1)} %get-tuple-element.50.old, ...), custom_call_target="tpu_custom_call" | custom-call | tf_op jit(solution)/shard_map/step/pallas_call | solution.py:823
  38.8 0.1 collective-permute-start.4
  38.9 2.0 %collective-permute-start.5 = (f32[96,128]{1,0:T(8,128)S(1)}, f32[96,128]{1,0:T(8,128)S(1)}, u32[]{:S(2)}, u32[]{:S(2)}) collective-permute-start(f32[96,128]{1,0:T(8,128)S(1)} %get-tuple-element.63), channel_id=1, source_target_pairs={{0,120},{8,16},{16,8},{24,32},{32,24},{40,48},{48,40},{56,64},{64,... | collective-permute-start | bytes 147464 | tf_op jit(solution)/shard_map/ppermute | solution.py:703
  40.8 0.0 collective-permute-done.4.even_in
  40.8 4.2 %collective-permute-done.5.odd_in = f32[96,128]{1,0:T(8,128)S(1)} collective-permute-done((f32[96,128]{1,0:T(8,128)S(1)}, f32[96,128]{1,0:T(8,128)S(1)}, u32[]{:S(2)}, u32[]{:S(2)}) %collective-permute-start.5) | collective-permute-done | bytes 49184 | tf_op jit(solution)/shard_map/ppermute | solution.py:703
  45.0 0.2 middle.5
  45.2 0.1 collective-permute-start.6
  45.2 5.7 %collective-permute-start.7 = (f32[64,128]{1,0:T(8,128)S(1)}, f32[64,128]{1,0:T(8,128)S(1)}, u32[]{:S(2)}, u32[]{:S(2)}) collective-permute-start(f32[64,128]{1,0:T(8,128)S(1)} %get-tuple-element.66), channel_id=1, source_target_pairs={{1,2},{2,1},{3,4},{4,3},{5,6},{6,5},{9,10},{10,9},{11,12},{12,11},... | collective-permute-start | bytes 98312 | tf_op jit(solution)/shard_map/ppermute | solution.py:703
  50.9 0.0 collective-permute-done.6.even_in
  50.9 2.5 %collective-permute-done.7.odd_in = f32[64,128]{1,0:T(8,128)S(1)} collective-permute-done((f32[64,128]{1,0:T(8,128)S(1)}, f32[64,128]{1,0:T(8,128)S(1)}, u32[]{:S(2)}, u32[]{:S(2)}) %collective-permute-start.7) | collective-permute-done | bytes 32800 | tf_op jit(solution)/shard_map/ppermute | solution.py:703
  53.5 1.8 %step.4 = (f32[768,128]{1,0:T(8,128)S(1)}, f32[768,128]{1,0:T(8,128)S(1)}, f32[768,128]{1,0:T(8,128)S(1)}, f32[10,128]{1,0:T(8,128)S(1)}, f32[96,128]{1,0:T(8,128)S(1)}, /*index=5*/f32[96,128]{1,0:T(8,128)S(1)}) custom-call(s32[1]{0:T(128)} %bitcast.2.blk, s32[1]{0:T(128)} %bitcast.1.lat, f32[768,128]{1,0:T(8,128)S(1)} %get-tuple-element.64.old, ...), custom_call_target="tpu_custom_call" | custom-call | tf_op jit(solution)/shard_map/step/pallas_call | solution.py:823
  55.3 0.1 collective-permute-start.8
  55.4 0.4 collective-permute-start.9
  55.8 0.8 collective-permute-done.8.even_in
  56.6 4.5 %collective-permute-done.9.odd_in = f32[96,128]{1,0:T(8,128)S(1)} collective-permute-done((f32[96,128]{1,0:T(8,128)S(1)}, f32[96,128]{1,0:T(8,128)S(1)}, u32[]{:S(2)}, u32[]{:S(2)}) %collective-permute-start.9) | collective-permute-done | bytes 49184 | tf_op jit(solution)/shard_map/ppermute | solution.py:703
  61.1 0.2 middle.6
  61.3 0.1 collective-permute-start.10
  61.4 6.2 %collective-permute-start.11 = (f32[64,128]{1,0:T(8,128)S(1)}, f32[64,128]{1,0:T(8,128)S(1)}, u32[]{:S(2)}, u32[]{:S(2)}) collective-permute-start(f32[64,128]{1,0:T(8,128)S(1)} %get-tuple-element.74), channel_id=1, source_target_pairs={{1,2},{2,1},{3,4},{4,3},{5,6},{6,5},{9,10},{10,9},{11,12},{12,11},... | collective-permute-start | bytes 98312 | tf_op jit(solution)/shard_map/ppermute | solution.py:703
  67.5 0.0 collective-permute-done.10.even_in
  67.6 2.0 %collective-permute-done.11.odd_in = f32[64,128]{1,0:T(8,128)S(1)} collective-permute-done((f32[64,128]{1,0:T(8,128)S(1)}, f32[64,128]{1,0:T(8,128)S(1)}, u32[]{:S(2)}, u32[]{:S(2)}) %collective-permute-start.11) | collective-permute-done | bytes 32800 | tf_op jit(solution)/shard_map/ppermute | solution.py:703
  69.6 0.0 copy-start
  69.6 1.8 %step.5 = (f32[768,128]{1,0:T(8,128)S(1)}, f32[768,128]{1,0:T(8,128)S(1)}, f32[768,128]{1,0:T(8,128)S(1)}, f32[10,128]{1,0:T(8,128)S(1)}, f32[96,128]{1,0:T(8,128)S(1)}, /*index=5*/f32[96,128]{1,0:T(8,128)S(1)}) custom-call(s32[1]{0:T(128)} %bitcast.2.blk, s32[1]{0:T(128)} %bitcast.1.lat, f32[768,128]{1,0:T(8,128)S(1)} %get-tuple-element.72.old, ...), custom_call_target="tpu_custom_call" | custom-call | tf_op jit(solution)/shard_map/step/pallas_call | solution.py:823
  71.4 0.1 collective-permute-start.12
  71.5 0.1 collective-permute-start.13
  71.6 1.1 %collective-permute-done.12.even_in = f32[96,128]{1,0:T(8,128)S(1)} collective-permute-done((f32[96,128]{1,0:T(8,128)S(1)}, f32[96,128]{1,0:T(8,128)S(1)}, u32[]{:S(2)}, u32[]{:S(2)}) %collective-permute-start.12) | collective-permute-done | bytes 49184 | tf_op jit(solution)/shard_map/ppermute | solution.py:704
  72.7 4.8 %collective-permute-done.13.odd_in = f32[96,128]{1,0:T(8,128)S(1)} collective-permute-done((f32[96,128]{1,0:T(8,128)S(1)}, f32[96,128]{1,0:T(8,128)S(1)}, u32[]{:S(2)}, u32[]{:S(2)}) %collective-permute-start.13) | collective-permute-done | bytes 49184 | tf_op jit(solution)/shard_map/ppermute | solution.py:703
  77.6 0.2 middle.7
  77.7 0.1 collective-permute-start.14
  77.8 9.1 %collective-permute-start.15 = (f32[64,128]{1,0:T(8,128)S(1)}, f32[64,128]{1,0:T(8,128)S(1)}, u32[]{:S(2)}, u32[]{:S(2)}) collective-permute-start(f32[64,128]{1,0:T(8,128)S(1)} %get-tuple-element.82), channel_id=1, source_target_pairs={{1,2},{2,1},{3,4},{4,3},{5,6},{6,5},{9,10},{10,9},{11,12},{12,11},... | collective-permute-start | bytes 98312 | tf_op jit(solution)/shard_map/ppermute | solution.py:703
  86.9 3.7 %inner.1.table_in = f32[9984,128]{1,0:T(8,128)S(1)} custom-call(s32[16000]{0:T(1024)} %bitcast.13, f32[768,128]{1,0:T(8,128)S(1)} %get-tuple-element.77.old.balance, f32[128,128]{1,0:T(8,128)S(1)} %get-tuple-element.53.inverse, f32[768,128]{1,0:T(8,128)S(1)} %get-tuple-element.83.motion_in, f32[768,128]{1,0:T(8,128)S(1)} %get-tuple-element.84.speed_in), custom_call_target="tpu_custom_call" | custom-call | tf_op jit(solution)/shard_map/inner/pallas_call | solution.py:856
  90.7 0.0 copy-done
  90.7 0.9 spectrum.1
  91.6 3.5 %outer.1.table_in = f32[9984,128]{1,0:T(8,128)S(1)} custom-call(s32[16000]{0:T(1024)} %bitcast.14, f32[768,128]{1,0:T(8,128)S(1)} %get-tuple-element.80.balance.old, f32[128,128]{1,0:T(8,128)S(1)} %get-tuple-element.53.inverse, f32[768,128]{1,0:T(8,128)S(1)} %get-tuple-element.83.motion_in, ...), custom_call_target="tpu_custom_call", output_to_operand_aliasing={{}: (5, {})} | custom-call | tf_op jit(solution)/shard_map/outer/pallas_call | solution.py:875
  95.1 0.0 collective-permute-done.14.even_in
  95.1 0.0 collective-permute-done.15.odd_in
  95.1 6.1 %last.1 = (f32[3,2,9945]{2,1,0:T(2,128)}, f32[3,2,9945]{2,1,0:T(2,128)}, f32[9984,128]{1,0:T(8,128)S(1)}) custom-call(s32[16000]{0:T(1024)} %bitcast.15, s32[1]{0:T(128)} %bitcast.1.lat, f32[768,128]{1,0:T(8,128)S(1)} %get-tuple-element.80.balance.old, f32[64,128]{1,0:T(8,128)S(1)} %collective-permute-done.14.even_in, ...), custom_call_target="tpu_custom_call", output_to_operand_aliasing={{2}: (8, {})} | custom-call | tf_op jit(solution)/shard_map/last/pallas_call | solution.py:894
Async XLA Ops:
  17.4 5.2 %collective-permute-start = (f32[96,128]{1,0:T(8,128)}, f32[96,128]{1,0:T(8,128)}, u32[]{:S(2)}, u32[]{:S(2)}) collective-permute-start(f32[96,128]{1,0:T(8,128)} %get-tuple-element.48), channel_id=1, source_target_pairs={{0,8},{8,0},{16,24},{24,16},{32,40},{40,32},{48,56},{56,48},{64,72... | collective-permute-start | bytes 147464 | tf_op jit(solution)/shard_map/ppermute | solution.py:704
  17.5 7.2 %collective-permute-start.1 = (f32[96,128]{1,0:T(8,128)}, f32[96,128]{1,0:T(8,128)}, u32[]{:S(2)}, u32[]{:S(2)}) collective-permute-start(f32[96,128]{1,0:T(8,128)} %get-tuple-element.49), channel_id=1, source_target_pairs={{0,120},{8,16},{16,8},{24,32},{32,24},{40,48},{48,40},{56,64},{64,... | collective-permute-start | bytes 147464 | tf_op jit(solution)/shard_map/ppermute | solution.py:703
  25.8 5.8 %collective-permute-start.2 = (f32[64,128]{1,0:T(8,128)S(1)}, f32[64,128]{1,0:T(8,128)S(1)}, u32[]{:S(2)}, u32[]{:S(2)}) collective-permute-start(f32[64,128]{1,0:T(8,128)S(1)} %get-tuple-element.51), channel_id=1, source_target_pairs={{0,1},{1,0},{2,3},{3,2},{4,5},{5,4},{6,7},{7,6},{8,9},{9,8},{10,11... | collective-permute-start | bytes 98312 | tf_op jit(solution)/shard_map/ppermute | solution.py:704
  28.7 8.2 %collective-permute-start.3 = (f32[64,128]{1,0:T(8,128)S(1)}, f32[64,128]{1,0:T(8,128)S(1)}, u32[]{:S(2)}, u32[]{:S(2)}) collective-permute-start(f32[64,128]{1,0:T(8,128)S(1)} %get-tuple-element.52), channel_id=1, source_target_pairs={{1,2},{2,1},{3,4},{4,3},{5,6},{6,5},{9,10},{10,9},{11,12},{12,11},... | collective-permute-start | bytes 98312 | tf_op jit(solution)/shard_map/ppermute | solution.py:703
  38.8 2.1 %collective-permute-start.4 = (f32[96,128]{1,0:T(8,128)S(1)}, f32[96,128]{1,0:T(8,128)S(1)}, u32[]{:S(2)}, u32[]{:S(2)}) collective-permute-start(f32[96,128]{1,0:T(8,128)S(1)} %get-tuple-element.62), channel_id=1, source_target_pairs={{0,8},{8,0},{16,24},{24,16},{32,40},{40,32},{48,56},{56,48},{64,72... | collective-permute-start | bytes 147464 | tf_op jit(solution)/shard_map/ppermute | solution.py:704
  38.9 6.1 %collective-permute-start.5 = (f32[96,128]{1,0:T(8,128)S(1)}, f32[96,128]{1,0:T(8,128)S(1)}, u32[]{:S(2)}, u32[]{:S(2)}) collective-permute-start(f32[96,128]{1,0:T(8,128)S(1)} %get-tuple-element.63), channel_id=1, source_target_pairs={{0,120},{8,16},{16,8},{24,32},{32,24},{40,48},{48,40},{56,64},{64,... | collective-permute-start | bytes 147464 | tf_op jit(solution)/shard_map/ppermute | solution.py:703
  45.2 5.8 %collective-permute-start.6 = (f32[64,128]{1,0:T(8,128)S(1)}, f32[64,128]{1,0:T(8,128)S(1)}, u32[]{:S(2)}, u32[]{:S(2)}) collective-permute-start(f32[64,128]{1,0:T(8,128)S(1)} %get-tuple-element.65), channel_id=1, source_target_pairs={{0,1},{1,0},{2,3},{3,2},{4,5},{5,4},{6,7},{7,6},{8,9},{9,8},{10,11... | collective-permute-start | bytes 98312 | tf_op jit(solution)/shard_map/ppermute | solution.py:704
  45.2 8.2 %collective-permute-start.7 = (f32[64,128]{1,0:T(8,128)S(1)}, f32[64,128]{1,0:T(8,128)S(1)}, u32[]{:S(2)}, u32[]{:S(2)}) collective-permute-start(f32[64,128]{1,0:T(8,128)S(1)} %get-tuple-element.66), channel_id=1, source_target_pairs={{1,2},{2,1},{3,4},{4,3},{5,6},{6,5},{9,10},{10,9},{11,12},{12,11},... | collective-permute-start | bytes 98312 | tf_op jit(solution)/shard_map/ppermute | solution.py:703
  55.3 1.3 %collective-permute-start.8 = (f32[96,128]{1,0:T(8,128)S(1)}, f32[96,128]{1,0:T(8,128)S(1)}, u32[]{:S(2)}, u32[]{:S(2)}) collective-permute-start(f32[96,128]{1,0:T(8,128)S(1)} %get-tuple-element.70), channel_id=1, source_target_pairs={{0,8},{8,0},{16,24},{24,16},{32,40},{40,32},{48,56},{56,48},{64,72... | collective-permute-start | bytes 147464 | tf_op jit(solution)/shard_map/ppermute | solution.py:704
  55.4 5.7 %collective-permute-start.9 = (f32[96,128]{1,0:T(8,128)S(1)}, f32[96,128]{1,0:T(8,128)S(1)}, u32[]{:S(2)}, u32[]{:S(2)}) collective-permute-start(f32[96,128]{1,0:T(8,128)S(1)} %get-tuple-element.71), channel_id=1, source_target_pairs={{0,120},{8,16},{16,8},{24,32},{32,24},{40,48},{48,40},{56,64},{64,... | collective-permute-start | bytes 147464 | tf_op jit(solution)/shard_map/ppermute | solution.py:703
  61.3 6.3 %collective-permute-start.10 = (f32[64,128]{1,0:T(8,128)S(1)}, f32[64,128]{1,0:T(8,128)S(1)}, u32[]{:S(2)}, u32[]{:S(2)}) collective-permute-start(f32[64,128]{1,0:T(8,128)S(1)} %get-tuple-element.73), channel_id=1, source_target_pairs={{0,1},{1,0},{2,3},{3,2},{4,5},{5,4},{6,7},{7,6},{8,9},{9,8},{10,11... | collective-permute-start | bytes 98312 | tf_op jit(solution)/shard_map/ppermute | solution.py:704
  61.4 8.2 %collective-permute-start.11 = (f32[64,128]{1,0:T(8,128)S(1)}, f32[64,128]{1,0:T(8,128)S(1)}, u32[]{:S(2)}, u32[]{:S(2)}) collective-permute-start(f32[64,128]{1,0:T(8,128)S(1)} %get-tuple-element.74), channel_id=1, source_target_pairs={{1,2},{2,1},{3,4},{4,3},{5,6},{6,5},{9,10},{10,9},{11,12},{12,11},... | collective-permute-start | bytes 98312 | tf_op jit(solution)/shard_map/ppermute | solution.py:703
  69.6 21.1 %copy-start = (bf16[640,128]{1,0:T(8,128)(2,1)S(1)}, bf16[640,128]{1,0:T(8,128)(2,1)}, u32[]{:S(2)}) copy-start(bf16[640,128]{1,0:T(8,128)(2,1)} %constant.23.clone.wide) | copy-start | bytes 491524
  71.4 1.3 %collective-permute-start.12 = (f32[96,128]{1,0:T(8,128)S(1)}, f32[96,128]{1,0:T(8,128)S(1)}, u32[]{:S(2)}, u32[]{:S(2)}) collective-permute-start(f32[96,128]{1,0:T(8,128)S(1)} %get-tuple-element.78), channel_id=1, source_target_pairs={{0,8},{8,0},{16,24},{24,16},{32,40},{40,32},{48,56},{56,48},{64,72... | collective-permute-start | bytes 147464 | tf_op jit(solution)/shard_map/ppermute | solution.py:704
  71.5 6.1 %collective-permute-start.13 = (f32[96,128]{1,0:T(8,128)S(1)}, f32[96,128]{1,0:T(8,128)S(1)}, u32[]{:S(2)}, u32[]{:S(2)}) collective-permute-start(f32[96,128]{1,0:T(8,128)S(1)} %get-tuple-element.79), channel_id=1, source_target_pairs={{0,120},{8,16},{16,8},{24,32},{32,24},{40,48},{48,40},{56,64},{64,... | collective-permute-start | bytes 147464 | tf_op jit(solution)/shard_map/ppermute | solution.py:703
  77.7 17.3 %collective-permute-start.14 = (f32[64,128]{1,0:T(8,128)S(1)}, f32[64,128]{1,0:T(8,128)S(1)}, u32[]{:S(2)}, u32[]{:S(2)}) collective-permute-start(f32[64,128]{1,0:T(8,128)S(1)} %get-tuple-element.81), channel_id=1, source_target_pairs={{0,1},{1,0},{2,3},{3,2},{4,5},{5,4},{6,7},{7,6},{8,9},{9,8},{10,11... | collective-permute-start | bytes 98312 | tf_op jit(solution)/shard_map/ppermute | solution.py:704
  77.8 17.3 %collective-permute-start.15 = (f32[64,128]{1,0:T(8,128)S(1)}, f32[64,128]{1,0:T(8,128)S(1)}, u32[]{:S(2)}, u32[]{:S(2)}) collective-permute-start(f32[64,128]{1,0:T(8,128)S(1)} %get-tuple-element.82), channel_id=1, source_target_pairs={{1,2},{2,1},{3,4},{4,3},{5,6},{6,5},{9,10},{10,9},{11,12},{12,11},... | collective-permute-start | bytes 98312 | tf_op jit(solution)/shard_map/ppermute | solution.py:703

commit v2 on v1

--- a/solution.py
+++ b/solution.py
@@ -16,12 +16,13 @@
 EVENTS = 32
 STEP_TOTAL = 4
 NXN = 9
-NYN = 17
 NODES_DEV = 9945
 NODE_BLOCKS = 78
 LINE = 72
 COMPS = 40
-SLOTS = 4
+PARTS = 6
+PART = 13 * 128
+REST = NODES_DEV - (PARTS - 1) * PART
 
 
 bf16 = jnp.bfloat16
@@ -109,28 +110,34 @@
     return pl.BlockSpec(memory_space=pltpu.SMEM)
 
 
-def start_pairs(numbers_hbm, chunks, sems, rounds, slots, pair_of):
+BOTH = (0, 1)
+ALL_ROWS = (0, 1, 2, 3)
+
+
+def start_pairs(numbers_hbm, chunks, sems, rounds, pairs):
     def fetch(index, slot):
-        a, b = pair_of(index, slot)
+        a, b = pairs[slot][0](index), pairs[slot][1]
         start = pl.multiple_of(128 * (25 * a + 5 * b), 128)
         return pltpu.make_async_copy(
-            numbers_hbm.at[pl.ds(start, 512)], chunks.at[slot], sems.at[slot]
-        )
-
-    for slot in range(slots):
+            numbers_hbm.at[pl.ds(start, 640)], chunks.at[pl.ds(640 * slot, 640)], sems.at[slot]
+        )
+
+    for slot in range(len(pairs)):
         fetch(jnp.int32(0), slot).start()
 
-    def visit_pairs(pair_places, visit):
+    def visit_pairs(pair_places, visit, between=None):
         def one_round(index, carry):
-            for slot in range(slots):
-                a, b = pair_of(index, slot)
+            for slot, (a_of, b, columns, rows) in enumerate(pairs):
+                a = a_of(index)
                 fetch(index, slot).wait()
-                for c in range(4):
+                for c in range(5):
+                    if between is not None and c in (0, 2):
+                        between(index, slot, c // 2)
                     places = pair_places(a, b, c)
-                    for ex in range(EXB):
-                        for ey in range(EYL):
-                            for ez in range(EZ):
-                                node = chunks[slot, 128 * c + 64 * ex + 16 * ey + ez]
+                    for ex in columns:
+                        for ey in rows:
+                            for ez in range(EZ - 1 if c == 4 else 0, EZ):
+                                node = chunks[640 * slot + 128 * c + 64 * ex + 16 * ey + ez]
                                 visit(places, c, ex, ey, ez, node)
                 if rounds > 1:
 
@@ -140,44 +147,37 @@
 
             return carry
 
-        lax.fori_loop(0, rounds, one_round, 0)
+        if rounds > 1:
+            lax.fori_loop(0, rounds, one_round, 0)
+        else:
+            one_round(jnp.int32(0), 0)
 
     return visit_pairs
 
 
-def visit_line(numbers, ix, iy, points, pair_places, visit):
-    ex = jnp.minimum(lax.shift_right_logical(ix, 2), EXB - 1)
-    ey = jnp.minimum(lax.shift_right_logical(iy, 2), EYL - 1)
-    a, b = ix - 4 * ex, iy - 4 * ey
-    start = 3200 * a + 640 * b + 64 * ex + 16 * ey
-    for c in points:
-        places = pair_places(a, b, c)
-        for ez in range(EZ - 1 if c == 4 else 0, EZ):
-            visit(places, c, ex, ey, ez, numbers[start + 128 * c + ez])
-
-
-def visit_far(numbers, plane_rows, last_row, top_rows, pair_places, visit):
-    first, count = plane_rows
-
-    def plane_line(index, carry):
-        visit_line(numbers, jnp.int32(NXN - 1), index + first, range(4), pair_places, visit)
-        return carry
-
-    lax.fori_loop(0, count, plane_line, 0)
-    if last_row:
-
-        def row_line(ix, carry):
-            visit_line(numbers, ix, jnp.int32(NYN - 1), range(4), pair_places, visit)
-            return carry
-
-        lax.fori_loop(0, NXN, row_line, 0)
-
-    def top(ix, carry):
-        for iy in top_rows:
-            visit_line(numbers, ix, jnp.int32(iy), (4,), pair_places, visit)
-        return carry
-
-    lax.fori_loop(0, NXN, top, 0)
+def fixed(value):
+    return lambda index: jnp.int32(value)
+
+
+def off_first(b):
+    return ALL_ROWS if b > 0 else ALL_ROWS[1:]
+
+
+MAIN_PAIRS = tuple((lambda index: index, b, BOTH, ALL_ROWS) for b in range(4))
+FAR_PAIRS = (
+    tuple((fixed(4), b, (1,), ALL_ROWS) for b in range(4))
+    + tuple((fixed(a), 4, BOTH, (3,)) for a in range(4))
+    + ((fixed(4), 4, (1,), (3,)),)
+)
+INNER_PAIRS = tuple((lambda index: index + 1, b, BOTH, off_first(b)) for b in range(4))
+OUTER_PAIRS = tuple((fixed(0), b, BOTH, off_first(b)) for b in range(4)) + tuple(
+    (fixed(4), b, (1,), off_first(b)) for b in range(4)
+)
+LAST_PAIRS = (
+    tuple((fixed(a), 0, BOTH, (0,)) for a in range(4))
+    + ((fixed(4), 0, (1,), (0,)),)
+    + FAR_PAIRS[4:]
+)
 
 
 def for_blocks(count, unroll, body):
@@ -218,8 +218,10 @@
     mixing,
     rows,
     table,
-    lines,
-    numbers,
+    lines_0,
+    lines_1,
+    lines_2,
+    lines_3,
     sources,
     displacement,
     velocity,
@@ -232,18 +234,20 @@
     sems,
     chunks,
     chunk_sems,
+    far_chunks,
+    far_sems,
 ):
+    lines = (lines_0, lines_1, lines_2, lines_3)
     copies = [
         pltpu.make_async_copy(source, target, sems.at[position])
         for position, (source, target) in enumerate(
             (
                 (frequency_hbm, frequency),
                 (pulses_hbm, pulses),
-                (sources_hbm, sources),
                 (displacement_hbm, displacement),
                 (velocity_hbm, velocity),
                 (mass_hbm, mass),
-                (numbers_hbm, numbers),
+                (sources_hbm, sources),
                 (shear_hbm, shear),
                 (lame_hbm, lame),
                 (weight_hbm, weight),
@@ -252,11 +256,11 @@
             )
         )
     ]
+
     for copy in copies:
         copy.start()
-    visit_pairs = start_pairs(
-        numbers_hbm, chunks, chunk_sems, 4, 4, lambda index, slot: (index, slot)
-    )
+    visit_far = start_pairs(numbers_hbm, far_chunks, far_sems, 1, FAR_PAIRS)
+    visit_pairs = start_pairs(numbers_hbm, chunks, chunk_sems, 4, MAIN_PAIRS)
     for copy in copies[0:2]:
         copy.wait()
     index = lax.broadcasted_iota(jnp.int32, (NFREQ, EVENTS), 0)
@@ -268,69 +272,98 @@
             for q in range(3):
                 row = 6 * k + 2 * q + s
                 mixing[row : row + 1, EVENTS * q : EVENTS * (q + 1)] = wavelet[k : k + 1]
-    for copy in copies[3:6]:
+    for copy in copies[2:5]:
         copy.wait()
     for q in range(3):
         rows[24 + 2 * q : 26 + 2 * q, 0:NODES_DEV] = displacement[q]
         rows[32 + 2 * q : 34 + 2 * q, 0:NODES_DEV] = velocity[q]
     rows[38:39, 0:NODES_DEV] = mass[...].reshape(1, NODES_DEV)
-    copies[2].wait()
-    flat = sources[...].reshape(3 * EVENTS, NODES_DEV)
-    rows[0:24, 0:NODES_DEV] = jnp.dot(
-        mixing[...].astype(bf16), flat, preferred_element_type=f32
+    mixed_events = mixing[...].astype(bf16)
+    copies[5].wait()
+
+    def force_rows(part):
+        columns = pl.ds(pl.multiple_of(part * PART, 128), PART)
+        flat = sources[:, :, columns].reshape(3 * EVENTS, PART)
+        rows[0:24, columns] = jnp.dot(mixed_events, flat, preferred_element_type=f32)
+
+    def node_rows(part):
+        for block in range(PART // 128):
+            start = pl.multiple_of(part * PART + block * 128, 128)
+            block_rows = rows[:, pl.ds(start, 128)]
+            filler = jnp.zeros((128 - 3 * COMPS, 128), f32)
+            table[pl.ds(start, 128), :] = jnp.concatenate(
+                [block_rows, block_rows, block_rows, filler], axis=0
+            ).T
+
+    force_rows(0)
+
+    def one_part(part, carry):
+        node_rows(part - 1)
+        force_rows(part)
+        return carry
+
+    lax.fori_loop(1, PARTS - 1, one_part, 0)
+    node_rows(PARTS - 2)
+    flat = sources[:, :, NODES_DEV - REST :].reshape(3 * EVENTS, REST)
+    rows[0:24, NODES_DEV - REST : NODES_DEV] = jnp.dot(
+        mixed_events, flat, preferred_element_type=f32
     )
-
-    def transpose_block(block):
-        start = pl.multiple_of(block * 128, 128)
-        block_rows = rows[:, pl.ds(start, 128)]
-        filler = jnp.zeros((128 - 3 * COMPS, 128), f32)
-        table[pl.ds(start, 128), :] = jnp.concatenate(
-            [block_rows, block_rows, block_rows, filler], axis=0
-        ).T
-
-    for_blocks(NODE_BLOCKS, 6, transpose_block)
+    node_rows(PARTS - 1)
     for copy in copies[6:]:
         copy.wait()
 
     def line_places(a, b, c):
-        return (a * NYN + b) * LINE + c
-
-    def gather_node(place, c, ex, ey, ez, node):
+        return lines[b % 4], (a * 5 + b // 4) * LINE + c
+
+    def gather_node(places, c, ex, ey, ez, node):
         del c
-        at = place + ((4 * ex * NYN + 4 * ey) * LINE + 4 * ez)
-        lines[pl.ds(at, 1), :] = table[pl.ds(node, 1), :]
-
-    visit_pairs(line_places, gather_node)
-    visit_far(numbers, (0, NYN - 1), True, range(NYN), line_places, gather_node)
+        target, place = places
+        at = place + ((20 * ex + ey) * LINE + 4 * ez)
+        target[pl.ds(at, 1), :] = table[pl.ds(node, 1), :]
 
     lanes = lanes_of(128)
 
-    def element_rows(pair):
-        a = lax.shift_right_logical(pair * 13, 6)
-        b = pair - 5 * a
-        for group in ((0, 1, 2), (3, 4)):
-            mixed = None
-            for position, c in reversed(list(enumerate(group))):
-                pieces = []
-                for ex in range(EXB):
-                    for ey in range(EYL):
-                        line = (4 * ex + a) * NYN + 4 * ey + b
-                        pieces.append(lines[pl.ds(line * LINE + c, EZ, stride=4), :])
-                whole = jnp.concatenate(pieces, axis=0)
-                if mixed is None:
-                    mixed = whole
-                else:
-                    mixed = jnp.where(lanes < COMPS * (position + 1), whole, mixed)
-            turned = mixed.T
-            for position, c in enumerate(group):
-                point = pair * 5 + c
-                base = COMPS * position
-                force_out[pl.ds(point, 24, stride=128), :] = turned[base : base + 24]
-                motion_out[pl.ds(point, 6, stride=128), :] = turned[base + 24 : base + 30]
-                speed_out[pl.ds(point, 6, stride=128), :] = turned[base + 32 : base + 38]
-                inverse_out[pl.ds(point, 1), :] = 1.0 / turned[base + 38 : base + 39]
-
-    for_blocks(25, 1, element_rows)
+    def element_rows(a, b, part):
+        group = ((0, 1, 2), (3, 4))[part]
+        mixed = None
+        for position, c in reversed(list(enumerate(group))):
+            pieces = []
+            for ex in range(EXB):
+                for ey in range(EYL):
+                    line = (4 * ex + a) * 5 + ey + b // 4
+                    pieces.append(lines[b % 4][pl.ds(line * LINE + c, EZ, stride=4), :])
+            whole = jnp.concatenate(pieces, axis=0)
+            if mixed is None:
+                mixed = whole
+            else:
+                mixed = jnp.where(lanes < COMPS * (position + 1), whole, mixed)
+        turned = mixed.T
+        for position, c in enumerate(group):
+            point = 25 * a + 5 * b + c
+            base = COMPS * position
+            force_out[pl.ds(point, 24, stride=128), :] = turned[base : base + 24]
+            motion_out[pl.ds(point, 6, stride=128), :] = turned[base + 24 : base + 30]
+            speed_out[pl.ds(point, 6, stride=128), :] = turned[base + 32 : base + 38]
+            inverse_out[pl.ds(point, 1), :] = 1.0 / turned[base + 38 : base + 39]
+
+    def rows_before(index, slot, part):
+        if slot == 0:
+            element_rows(jnp.maximum(index - 1, 0), 3, part)
+        else:
+            element_rows(index, slot - 1, part)
+
+    visit_far(line_places, gather_node)
+    visit_pairs(line_places, gather_node, rows_before)
+
+    def far_rows(a, carry):
+        for part in range(2):
+            element_rows(a, 4, part)
+        return carry
+
+    lax.fori_loop(0, 5, far_rows, 0)
+    for a, b in ((3, 3), (4, 0), (4, 1), (4, 2), (4, 3)):
+        for part in range(2):
+            element_rows(a, b, part)
     for point in range(125, 128):
         force_out[pl.ds(point, 24, stride=128), :] = jnp.zeros((24, 128), f32)
         motion_out[pl.ds(point, 6, stride=128), :] = jnp.zeros((6, 128), f32)
@@ -591,9 +624,7 @@
 def inner_kernel(
     numbers_hbm, balance, inverse, motion_in, speed_in, table, state, points, chunks, sems
 ):
-    visit_pairs = start_pairs(
-        numbers_hbm, chunks, sems, 3, 3, lambda index, slot: (index + 1, slot + 1)
-    )
+    visit_pairs = start_pairs(numbers_hbm, chunks, sems, 3, INNER_PAIRS)
     state_of(balance, inverse, motion_in, speed_in, state)
     visit_pairs(*scatter_to(table, state, points))
 
@@ -610,20 +641,11 @@
     points,
     chunks,
     sems,
-    numbers,
-    whole_sem,
 ):
     del table_in
-    whole = pltpu.make_async_copy(numbers_hbm, numbers, whole_sem)
-    whole.start()
-    visit_pairs = start_pairs(
-        numbers_hbm, chunks, sems, 1, 3, lambda index, slot: (index, slot + 1)
-    )
+    visit_pairs = start_pairs(numbers_hbm, chunks, sems, 1, OUTER_PAIRS)
     state_of(balance, inverse, motion_in, speed_in, state)
-    places, visit = scatter_to(table, state, points)
-    visit_pairs(places, visit)
-    whole.wait()
-    visit_far(numbers, (1, NYN - 2), False, range(1, NYN - 1), places, visit)
+    visit_pairs(*scatter_to(table, state, points))
 
 
 def last_kernel(
@@ -644,20 +666,13 @@
     points,
     chunks,
     sems,
-    numbers,
-    whole_sem,
 ):
     del table_in
-    whole = pltpu.make_async_copy(numbers_hbm, numbers, whole_sem)
-    whole.start()
-    visit_pairs = start_pairs(numbers_hbm, chunks, sems, 1, 4, lambda index, slot: (slot, index))
+    visit_pairs = start_pairs(numbers_hbm, chunks, sems, 1, LAST_PAIRS)
     balance[...] = old[...]
     add_lat(balance, lat, even_in, odd_in)
     state_of(balance, inverse, motion_in, speed_in, state)
-    places, visit = scatter_to(table, state, points)
-    visit_pairs(places, visit)
-    whole.wait()
-    visit_far(numbers, (0, 1), True, (0, NYN - 1), places, visit)
+    visit_pairs(*scatter_to(table, state, points))
 
     def turned(start):
         values = table[pl.ds(start, 128), :].T
@@ -703,6 +718,10 @@
     odd = lax.ppermute(odd, axis, odd_pairs)
     even = lax.ppermute(even, axis, even_pairs)
     return odd, even
+
+
+def chunk_scratch(pairs):
+    return [pltpu.SMEM((640 * len(pairs),), jnp.int32), pltpu.SemaphoreType.DMA((len(pairs),))]
 
 
 def limit(mebibytes):
@@ -768,8 +787,7 @@
             pltpu.VMEM((24, 3 * EVENTS), f32),
             pltpu.VMEM((COMPS, NODE_BLOCKS * 128), f32),
             pltpu.VMEM((NODE_BLOCKS * 128, 128), f32),
-            pltpu.VMEM((NXN * NYN * LINE, 128), f32),
-            pltpu.SMEM((125 * 128,), jnp.int32),
+            *[pltpu.VMEM((NXN * 5 * LINE, 128), f32)] * 4,
             pltpu.VMEM((3, EVENTS, NODES_DEV), bf16),
             pltpu.VMEM((3, 2, NODES_DEV), f32),
             pltpu.VMEM((3, 2, NODES_DEV), f32),
@@ -779,9 +797,9 @@
             pltpu.VMEM((128, 128), f32),
             pltpu.VMEM((8, NFREQ), bf16),
             pltpu.VMEM((2, EVENTS), jnp.int32),
-            pltpu.SemaphoreType.DMA((12,)),
-            pltpu.SMEM((SLOTS, 512), jnp.int32),
-            pltpu.SemaphoreType.DMA((SLOTS,)),
+            pltpu.SemaphoreType.DMA((11,)),
+            *chunk_scratch(MAIN_PAIRS),
+            *chunk_scratch(FAR_PAIRS),
         ],
         compiler_params=limit(24),
         name="gather",
@@ -811,13 +829,7 @@
     integrals = []
     numbers_hbm = pltpu.with_memory_space_constraint(numbers, pltpu.HBM)
     table_shape = kept(NODE_BLOCKS * 128, 128)
-    scatter_scratch = [
-        pltpu.VMEM((2048, 128), f32),
-        pltpu.VMEM((16 * 128, 128), f32),
-        pltpu.SMEM((SLOTS, 512), jnp.int32),
-        pltpu.SemaphoreType.DMA((SLOTS,)),
-    ]
-    whole_scratch = [pltpu.SMEM((125 * 128,), jnp.int32), pltpu.SemaphoreType.DMA]
+    scatter_scratch = [pltpu.VMEM((2048, 128), f32), pltpu.VMEM((16 * 128, 128), f32)]
     for step in range(STEP_TOTAL):
         if step > 0:
             balance, motion, speed, integral, even, odd = pl.pallas_call(
@@ -858,7 +870,7 @@
                 out_shape=table_shape,
                 in_specs=[hbm()] + [vmem()] * 4,
                 out_specs=vmem(),
-                scratch_shapes=scatter_scratch,
+                scratch_shapes=scatter_scratch + chunk_scratch(INNER_PAIRS),
                 compiler_params=limit(16),
                 name="inner",
             )(numbers_hbm, *hold(balance, inverse, motion, speed))
@@ -877,7 +889,7 @@
         out_shape=table_shape,
         in_specs=[hbm()] + [vmem()] * 5,
         out_specs=vmem(),
-        scratch_shapes=scatter_scratch + whole_scratch,
+        scratch_shapes=scatter_scratch + chunk_scratch(OUTER_PAIRS),
         input_output_aliases={5: 0},
         compiler_params=limit(16),
         name="outer",
@@ -896,7 +908,7 @@
         out_shape=(nodal, nodal, table_shape),
         in_specs=[hbm(), smem()] + [vmem()] * 7,
         out_specs=[vmem()] * 3,
-        scratch_shapes=[pltpu.VMEM((768, 128), f32)] + scatter_scratch + whole_scratch,
+        scratch_shapes=[pltpu.VMEM((768, 128), f32)] + scatter_scratch + chunk_scratch(LAST_PAIRS),
         input_output_aliases={8: 2},
         compiler_params=limit(16),
         name="last",

time: 102 us -> 97.5 us (0.956)
  Pallas kernels: 38 us -> 34 us
    pallas_call x1, Pallas kernels: 16.8 us -> 14.3 us  [local(): pl.pallas_call(gather_kernel, out_shape=(kept(24 * 128, 128), kept(768, 1...]
    pallas_call x1, Pallas kernels: 6.12 us -> 4.91 us  [local(): pl.pallas_call(last_kernel, out_shape=(nodal, nodal, table_shape), in_spe...]
where the time goes in v2:
time: 97.5 us; the launch traced here: 97.3 us
  starting transfers between devices  34.9 us (36%)
  Pallas kernels  34 us (35%)
  waiting for transfers between devices  27.3 us (28%)
  between operations  1.02 us (1%)
    ppermute x8, starting transfers between devices, exchange(): odd = lax.ppermute(odd, axis, odd_pairs)  31.3 us
    ppermute x8, waiting for transfers between devices, exchange(): odd = lax.ppermute(odd, axis, odd_pairs)  25.3 us
    pallas_call x1, Pallas kernels, local(): pl.pallas_call(gather_kernel, out_shape=(kept(24 * 128, 128), kept(768, 1...  14.3 us
    pallas_call x3, Pallas kernels, local(): pl.pallas_call(make_step_kernel(step), out_shape=(balance_shape, balance_...  5.48 us
    pallas_call x1, Pallas kernels, local(): pl.pallas_call(last_kernel, out_shape=(nodal, nodal, table_shape), in_spe...  4.91 us
    pallas_call x1, Pallas kernels, local(): pl.pallas_call(inner_kernel, out_shape=table_shape, in_specs=[hbm()] + [v...  4.27 us
    ppermute x8, starting transfers between devices, exchange(): even = lax.ppermute(even, axis, even_pairs)  3.58 us
    pallas_call x1, Pallas kernels, local(): pl.pallas_call(outer_kernel, out_shape=table_shape, in_specs=[hbm()] + [v...  2.61 us
  transfers between devices with their start and end apart: 16, of which 9 were waited for; matrix products, arithmetic and copies ran while one was open for 0% of the time, Pallas kernels for 8%

profile of v2, /device:TPU:6, one launch (start us, length us, event | category | flops | bytes accessed | tf_op | source)
XLA Modules:
  0.0 97.3 jit_solution(13588601682736780136)
XLA Ops:
  0.6 14.3 %gather.1 = (f32[3072,128]{1,0:T(8,128)S(1)}, f32[768,128]{1,0:T(8,128)S(1)}, f32[768,128]{1,0:T(8,128)S(1)}, f32[128,128]{1,0:T(8,128)S(1)}, f32[128,128]{1,0:T...) custom-call(s32[16000]{0:T(1024)} %bitcast.12, ...), custom_call_target="tpu_custom_call" | custom-call | tf_op jit(solution)/shard_map/gather/pallas_call | solution.py:768
  15.0 0.1 collective-permute-start
  15.1 5.2 %collective-permute-start.1 = (f32[96,128]{1,0:T(8,128)}, f32[96,128]{1,0:T(8,128)}, u32[]{:S(2)}, u32[]{:S(2)}) collective-permute-start(f32[96,128]{1,0:T(8,128)} %get-tuple-element.49), channel_id=1, source_target_pairs={{0,120},{8,16},{16,8},{24,32},{32,24},{40,48},{48,40},{56,64},{64,... | collective-permute-start | bytes 147464 | tf_op jit(solution)/shard_map/ppermute | solution.py:718
  20.2 0.0 collective-permute-done.even_in
  20.2 2.1 %collective-permute-done.1.odd_in = f32[96,128]{1,0:T(8,128)} collective-permute-done((f32[96,128]{1,0:T(8,128)}, f32[96,128]{1,0:T(8,128)}, u32[]{:S(2)}, u32[]{:S(2)}) %collective-permute-start.1) | collective-permute-done | bytes 49184 | tf_op jit(solution)/shard_map/ppermute | solution.py:718
  22.3 1.0 %middle.4 = (f32[768,128]{1,0:T(8,128)S(1)}, f32[64,128]{1,0:T(8,128)S(1)}, f32[64,128]{1,0:T(8,128)S(1)}) custom-call(s32[1]{0:T(128)} %bitcast.2.blk, s32[1]{0:T(128)} %bitcast.1.lat, f32[768,128]{1,0:T(8,128)S(1)} %get-tuple-element.47.old, f32[96,128]{1,0:T(8,128)} %collective-permute-done.even_in, f32[96,128]{1,0:T(8,128)} %collective-permute-done.1.odd_in), custom_call_target="tpu_custom_call" | custom-call | tf_op jit(solution)/shard_map/middle/pallas_call | solution.py:877
  23.3 3.0 %collective-permute-start.2 = (f32[64,128]{1,0:T(8,128)S(1)}, f32[64,128]{1,0:T(8,128)S(1)}, u32[]{:S(2)}, u32[]{:S(2)}) collective-permute-start(f32[64,128]{1,0:T(8,128)S(1)} %get-tuple-element.51), channel_id=1, source_target_pairs={{0,1},{1,0},{2,3},{3,2},{4,5},{5,4},{6,7},{7,6},{8,9},{9,8},{10,11... | collective-permute-start | bytes 98312 | tf_op jit(solution)/shard_map/ppermute | solution.py:719
  26.3 2.8 %collective-permute-start.3 = (f32[64,128]{1,0:T(8,128)S(1)}, f32[64,128]{1,0:T(8,128)S(1)}, u32[]{:S(2)}, u32[]{:S(2)}) collective-permute-start(f32[64,128]{1,0:T(8,128)S(1)} %get-tuple-element.52), channel_id=1, source_target_pairs={{1,2},{2,1},{3,4},{4,3},{5,6},{6,5},{9,10},{10,9},{11,12},{12,11},... | collective-permute-start | bytes 98312 | tf_op jit(solution)/shard_map/ppermute | solution.py:718
  29.1 0.0 collective-permute-done.2.even_in
  29.1 5.4 %collective-permute-done.3.odd_in = f32[64,128]{1,0:T(8,128)S(1)} collective-permute-done((f32[64,128]{1,0:T(8,128)S(1)}, f32[64,128]{1,0:T(8,128)S(1)}, u32[]{:S(2)}, u32[]{:S(2)}) %collective-permute-start.3) | collective-permute-done | bytes 32800 | tf_op jit(solution)/shard_map/ppermute | solution.py:718
  34.5 1.8 %step.3 = (f32[768,128]{1,0:T(8,128)S(1)}, f32[768,128]{1,0:T(8,128)S(1)}, f32[768,128]{1,0:T(8,128)S(1)}, f32[10,128]{1,0:T(8,128)S(1)}, f32[96,128]{1,0:T(8,128)S(1)}, /*index=5*/f32[96,128]{1,0:T(8,128)S(1)}) custom-call(s32[1]{0:T(128)} %bitcast.2.blk, s32[1]{0:T(128)} %bitcast.1.lat, f32[768,128]{1,0:T(8,128)S(1)} %get-tuple-element.50.old, ...), custom_call_target="tpu_custom_call" | custom-call | tf_op jit(solution)/shard_map/step/pallas_call | solution.py:835
  36.3 0.1 collective-permute-start.4
  36.4 2.0 %collective-permute-start.5 = (f32[96,128]{1,0:T(8,128)S(1)}, f32[96,128]{1,0:T(8,128)S(1)}, u32[]{:S(2)}, u32[]{:S(2)}) collective-permute-start(f32[96,128]{1,0:T(8,128)S(1)} %get-tuple-element.63), channel_id=1, source_target_pairs={{0,120},{8,16},{16,8},{24,32},{32,24},{40,48},{48,40},{56,64},{64,... | collective-permute-start | bytes 147464 | tf_op jit(solution)/shard_map/ppermute | solution.py:718
  38.4 0.0 collective-permute-done.4.even_in
  38.4 4.2 %collective-permute-done.5.odd_in = f32[96,128]{1,0:T(8,128)S(1)} collective-permute-done((f32[96,128]{1,0:T(8,128)S(1)}, f32[96,128]{1,0:T(8,128)S(1)}, u32[]{:S(2)}, u32[]{:S(2)}) %collective-permute-start.5) | collective-permute-done | bytes 49184 | tf_op jit(solution)/shard_map/ppermute | solution.py:718
  42.5 0.2 middle.5
  42.7 0.1 collective-permute-start.6
  42.8 5.7 %collective-permute-start.7 = (f32[64,128]{1,0:T(8,128)S(1)}, f32[64,128]{1,0:T(8,128)S(1)}, u32[]{:S(2)}, u32[]{:S(2)}) collective-permute-start(f32[64,128]{1,0:T(8,128)S(1)} %get-tuple-element.66), channel_id=1, source_target_pairs={{1,2},{2,1},{3,4},{4,3},{5,6},{6,5},{9,10},{10,9},{11,12},{12,11},... | collective-permute-start | bytes 98312 | tf_op jit(solution)/shard_map/ppermute | solution.py:718
  48.5 0.0 collective-permute-done.6.even_in
  48.5 2.5 %collective-permute-done.7.odd_in = f32[64,128]{1,0:T(8,128)S(1)} collective-permute-done((f32[64,128]{1,0:T(8,128)S(1)}, f32[64,128]{1,0:T(8,128)S(1)}, u32[]{:S(2)}, u32[]{:S(2)}) %collective-permute-start.7) | collective-permute-done | bytes 32800 | tf_op jit(solution)/shard_map/ppermute | solution.py:718
  51.0 1.8 %step.4 = (f32[768,128]{1,0:T(8,128)S(1)}, f32[768,128]{1,0:T(8,128)S(1)}, f32[768,128]{1,0:T(8,128)S(1)}, f32[10,128]{1,0:T(8,128)S(1)}, f32[96,128]{1,0:T(8,128)S(1)}, /*index=5*/f32[96,128]{1,0:T(8,128)S(1)}) custom-call(s32[1]{0:T(128)} %bitcast.2.blk, s32[1]{0:T(128)} %bitcast.1.lat, f32[768,128]{1,0:T(8,128)S(1)} %get-tuple-element.64.old, ...), custom_call_target="tpu_custom_call" | custom-call | tf_op jit(solution)/shard_map/step/pallas_call | solution.py:835
  52.9 0.1 collective-permute-start.8
  53.0 0.4 collective-permute-start.9
  53.3 0.8 collective-permute-done.8.even_in
  54.2 4.5 %collective-permute-done.9.odd_in = f32[96,128]{1,0:T(8,128)S(1)} collective-permute-done((f32[96,128]{1,0:T(8,128)S(1)}, f32[96,128]{1,0:T(8,128)S(1)}, u32[]{:S(2)}, u32[]{:S(2)}) %collective-permute-start.9) | collective-permute-done | bytes 49184 | tf_op jit(solution)/shard_map/ppermute | solution.py:718
  58.7 0.2 middle.6
  58.8 0.1 collective-permute-start.10
  58.9 6.3 %collective-permute-start.11 = (f32[64,128]{1,0:T(8,128)S(1)}, f32[64,128]{1,0:T(8,128)S(1)}, u32[]{:S(2)}, u32[]{:S(2)}) collective-permute-start(f32[64,128]{1,0:T(8,128)S(1)} %get-tuple-element.74), channel_id=1, source_target_pairs={{1,2},{2,1},{3,4},{4,3},{5,6},{6,5},{9,10},{10,9},{11,12},{12,11},... | collective-permute-start | bytes 98312 | tf_op jit(solution)/shard_map/ppermute | solution.py:718
  65.3 0.0 collective-permute-done.10.even_in
  65.3 1.8 %collective-permute-done.11.odd_in = f32[64,128]{1,0:T(8,128)S(1)} collective-permute-done((f32[64,128]{1,0:T(8,128)S(1)}, f32[64,128]{1,0:T(8,128)S(1)}, u32[]{:S(2)}, u32[]{:S(2)}) %collective-permute-start.11) | collective-permute-done | bytes 32800 | tf_op jit(solution)/shard_map/ppermute | solution.py:718
  67.1 0.0 copy-start
  67.1 1.8 %step.5 = (f32[768,128]{1,0:T(8,128)S(1)}, f32[768,128]{1,0:T(8,128)S(1)}, f32[768,128]{1,0:T(8,128)S(1)}, f32[10,128]{1,0:T(8,128)S(1)}, f32[96,128]{1,0:T(8,128)S(1)}, /*index=5*/f32[96,128]{1,0:T(8,128)S(1)}) custom-call(s32[1]{0:T(128)} %bitcast.2.blk, s32[1]{0:T(128)} %bitcast.1.lat, f32[768,128]{1,0:T(8,128)S(1)} %get-tuple-element.72.old, ...), custom_call_target="tpu_custom_call" | custom-call | tf_op jit(solution)/shard_map/step/pallas_call | solution.py:835
  69.0 0.1 collective-permute-start.12
  69.1 0.1 collective-permute-start.13
  69.2 1.1 %collective-permute-done.12.even_in = f32[96,128]{1,0:T(8,128)S(1)} collective-permute-done((f32[96,128]{1,0:T(8,128)S(1)}, f32[96,128]{1,0:T(8,128)S(1)}, u32[]{:S(2)}, u32[]{:S(2)}) %collective-permute-start.12) | collective-permute-done | bytes 49184 | tf_op jit(solution)/shard_map/ppermute | solution.py:719
  70.3 4.8 %collective-permute-done.13.odd_in = f32[96,128]{1,0:T(8,128)S(1)} collective-permute-done((f32[96,128]{1,0:T(8,128)S(1)}, f32[96,128]{1,0:T(8,128)S(1)}, u32[]{:S(2)}, u32[]{:S(2)}) %collective-permute-start.13) | collective-permute-done | bytes 49184 | tf_op jit(solution)/shard_map/ppermute | solution.py:718
  75.1 0.2 middle.7
  75.3 0.1 collective-permute-start.14
  75.4 8.9 %collective-permute-start.15 = (f32[64,128]{1,0:T(8,128)S(1)}, f32[64,128]{1,0:T(8,128)S(1)}, u32[]{:S(2)}, u32[]{:S(2)}) collective-permute-start(f32[64,128]{1,0:T(8,128)S(1)} %get-tuple-element.82), channel_id=1, source_target_pairs={{1,2},{2,1},{3,4},{4,3},{5,6},{6,5},{9,10},{10,9},{11,12},{12,11},... | collective-permute-start | bytes 98312 | tf_op jit(solution)/shard_map/ppermute | solution.py:718
  84.3 4.3 %inner.1.table_in = f32[9984,128]{1,0:T(8,128)S(1)} custom-call(s32[16000]{0:T(1024)} %bitcast.13, f32[768,128]{1,0:T(8,128)S(1)} %get-tuple-element.77.old.balance, f32[128,128]{1,0:T(8,128)S(1)} %get-tuple-element.53.inverse, f32[768,128]{1,0:T(8,128)S(1)} %get-tuple-element.83.motion_in, f32[768,128]{1,0:T(8,128)S(1)} %get-tuple-element.84.speed_in), custom_call_target="tpu_custom_call" | custom-call | tf_op jit(solution)/shard_map/inner/pallas_call | solution.py:868
  88.6 0.0 copy-done
  88.6 0.9 spectrum.1
  89.5 2.6 %outer.1.table_in = f32[9984,128]{1,0:T(8,128)S(1)} custom-call(s32[16000]{0:T(1024)} %bitcast.14, f32[768,128]{1,0:T(8,128)S(1)} %get-tuple-element.80.balance.old, f32[128,128]{1,0:T(8,128)S(1)} %get-tuple-element.53.inverse, f32[768,128]{1,0:T(8,128)S(1)} %get-tuple-element.83.motion_in, ...), custom_call_target="tpu_custom_call", output_to_operand_aliasing={{}: (5, {})} | custom-call | tf_op jit(solution)/shard_map/outer/pallas_call | solution.py:887
  92.2 0.0 collective-permute-done.14.even_in
  92.2 0.0 collective-permute-done.15.odd_in
  92.2 4.9 %last.1 = (f32[3,2,9945]{2,1,0:T(2,128)}, f32[3,2,9945]{2,1,0:T(2,128)}, f32[9984,128]{1,0:T(8,128)S(1)}) custom-call(s32[16000]{0:T(1024)} %bitcast.15, s32[1]{0:T(128)} %bitcast.1.lat, f32[768,128]{1,0:T(8,128)S(1)} %get-tuple-element.80.balance.old, f32[64,128]{1,0:T(8,128)S(1)} %collective-permute-done.14.even_in, ...), custom_call_target="tpu_custom_call", output_to_operand_aliasing={{2}: (8, {})} | custom-call | tf_op jit(solution)/shard_map/last/pallas_call | solution.py:906
Async XLA Ops:
  15.0 5.2 %collective-permute-start = (f32[96,128]{1,0:T(8,128)}, f32[96,128]{1,0:T(8,128)}, u32[]{:S(2)}, u32[]{:S(2)}) collective-permute-start(f32[96,128]{1,0:T(8,128)} %get-tuple-element.48), channel_id=1, source_target_pairs={{0,8},{8,0},{16,24},{24,16},{32,40},{40,32},{48,56},{56,48},{64,72... | collective-permute-start | bytes 147464 | tf_op jit(solution)/shard_map/ppermute | solution.py:719
  15.1 7.2 %collective-permute-start.1 = (f32[96,128]{1,0:T(8,128)}, f32[96,128]{1,0:T(8,128)}, u32[]{:S(2)}, u32[]{:S(2)}) collective-permute-start(f32[96,128]{1,0:T(8,128)} %get-tuple-element.49), channel_id=1, source_target_pairs={{0,120},{8,16},{16,8},{24,32},{32,24},{40,48},{48,40},{56,64},{64,... | collective-permute-start | bytes 147464 | tf_op jit(solution)/shard_map/ppermute | solution.py:718
  23.3 5.8 %collective-permute-start.2 = (f32[64,128]{1,0:T(8,128)S(1)}, f32[64,128]{1,0:T(8,128)S(1)}, u32[]{:S(2)}, u32[]{:S(2)}) collective-permute-start(f32[64,128]{1,0:T(8,128)S(1)} %get-tuple-element.51), channel_id=1, source_target_pairs={{0,1},{1,0},{2,3},{3,2},{4,5},{5,4},{6,7},{7,6},{8,9},{9,8},{10,11... | collective-permute-start | bytes 98312 | tf_op jit(solution)/shard_map/ppermute | solution.py:719
  26.3 8.2 %collective-permute-start.3 = (f32[64,128]{1,0:T(8,128)S(1)}, f32[64,128]{1,0:T(8,128)S(1)}, u32[]{:S(2)}, u32[]{:S(2)}) collective-permute-start(f32[64,128]{1,0:T(8,128)S(1)} %get-tuple-element.52), channel_id=1, source_target_pairs={{1,2},{2,1},{3,4},{4,3},{5,6},{6,5},{9,10},{10,9},{11,12},{12,11},... | collective-permute-start | bytes 98312 | tf_op jit(solution)/shard_map/ppermute | solution.py:718
  36.3 2.1 %collective-permute-start.4 = (f32[96,128]{1,0:T(8,128)S(1)}, f32[96,128]{1,0:T(8,128)S(1)}, u32[]{:S(2)}, u32[]{:S(2)}) collective-permute-start(f32[96,128]{1,0:T(8,128)S(1)} %get-tuple-element.62), channel_id=1, source_target_pairs={{0,8},{8,0},{16,24},{24,16},{32,40},{40,32},{48,56},{56,48},{64,72... | collective-permute-start | bytes 147464 | tf_op jit(solution)/shard_map/ppermute | solution.py:719
  36.4 6.1 %collective-permute-start.5 = (f32[96,128]{1,0:T(8,128)S(1)}, f32[96,128]{1,0:T(8,128)S(1)}, u32[]{:S(2)}, u32[]{:S(2)}) collective-permute-start(f32[96,128]{1,0:T(8,128)S(1)} %get-tuple-element.63), channel_id=1, source_target_pairs={{0,120},{8,16},{16,8},{24,32},{32,24},{40,48},{48,40},{56,64},{64,... | collective-permute-start | bytes 147464 | tf_op jit(solution)/shard_map/ppermute | solution.py:718
  42.7 5.8 %collective-permute-start.6 = (f32[64,128]{1,0:T(8,128)S(1)}, f32[64,128]{1,0:T(8,128)S(1)}, u32[]{:S(2)}, u32[]{:S(2)}) collective-permute-start(f32[64,128]{1,0:T(8,128)S(1)} %get-tuple-element.65), channel_id=1, source_target_pairs={{0,1},{1,0},{2,3},{3,2},{4,5},{5,4},{6,7},{7,6},{8,9},{9,8},{10,11... | collective-permute-start | bytes 98312 | tf_op jit(solution)/shard_map/ppermute | solution.py:719
  42.8 8.2 %collective-permute-start.7 = (f32[64,128]{1,0:T(8,128)S(1)}, f32[64,128]{1,0:T(8,128)S(1)}, u32[]{:S(2)}, u32[]{:S(2)}) collective-permute-start(f32[64,128]{1,0:T(8,128)S(1)} %get-tuple-element.66), channel_id=1, source_target_pairs={{1,2},{2,1},{3,4},{4,3},{5,6},{6,5},{9,10},{10,9},{11,12},{12,11},... | collective-permute-start | bytes 98312 | tf_op jit(solution)/shard_map/ppermute | solution.py:718
  52.9 1.3 %collective-permute-start.8 = (f32[96,128]{1,0:T(8,128)S(1)}, f32[96,128]{1,0:T(8,128)S(1)}, u32[]{:S(2)}, u32[]{:S(2)}) collective-permute-start(f32[96,128]{1,0:T(8,128)S(1)} %get-tuple-element.70), channel_id=1, source_target_pairs={{0,8},{8,0},{16,24},{24,16},{32,40},{40,32},{48,56},{56,48},{64,72... | collective-permute-start | bytes 147464 | tf_op jit(solution)/shard_map/ppermute | solution.py:719
  53.0 5.7 %collective-permute-start.9 = (f32[96,128]{1,0:T(8,128)S(1)}, f32[96,128]{1,0:T(8,128)S(1)}, u32[]{:S(2)}, u32[]{:S(2)}) collective-permute-start(f32[96,128]{1,0:T(8,128)S(1)} %get-tuple-element.71), channel_id=1, source_target_pairs={{0,120},{8,16},{16,8},{24,32},{32,24},{40,48},{48,40},{56,64},{64,... | collective-permute-start | bytes 147464 | tf_op jit(solution)/shard_map/ppermute | solution.py:718
  58.8 6.5 %collective-permute-start.10 = (f32[64,128]{1,0:T(8,128)S(1)}, f32[64,128]{1,0:T(8,128)S(1)}, u32[]{:S(2)}, u32[]{:S(2)}) collective-permute-start(f32[64,128]{1,0:T(8,128)S(1)} %get-tuple-element.73), channel_id=1, source_target_pairs={{0,1},{1,0},{2,3},{3,2},{4,5},{5,4},{6,7},{7,6},{8,9},{9,8},{10,11... | collective-permute-start | bytes 98312 | tf_op jit(solution)/shard_map/ppermute | solution.py:719
  58.9 8.2 %collective-permute-start.11 = (f32[64,128]{1,0:T(8,128)S(1)}, f32[64,128]{1,0:T(8,128)S(1)}, u32[]{:S(2)}, u32[]{:S(2)}) collective-permute-start(f32[64,128]{1,0:T(8,128)S(1)} %get-tuple-element.74), channel_id=1, source_target_pairs={{1,2},{2,1},{3,4},{4,3},{5,6},{6,5},{9,10},{10,9},{11,12},{12,11},... | collective-permute-start | bytes 98312 | tf_op jit(solution)/shard_map/ppermute | solution.py:718
  67.1 21.5 %copy-start = (bf16[640,128]{1,0:T(8,128)(2,1)S(1)}, bf16[640,128]{1,0:T(8,128)(2,1)}, u32[]{:S(2)}) copy-start(bf16[640,128]{1,0:T(8,128)(2,1)} %constant.23.clone.wide) | copy-start | bytes 491524
  69.0 1.3 %collective-permute-start.12 = (f32[96,128]{1,0:T(8,128)S(1)}, f32[96,128]{1,0:T(8,128)S(1)}, u32[]{:S(2)}, u32[]{:S(2)}) collective-permute-start(f32[96,128]{1,0:T(8,128)S(1)} %get-tuple-element.78), channel_id=1, source_target_pairs={{0,8},{8,0},{16,24},{24,16},{32,40},{40,32},{48,56},{56,48},{64,72... | collective-permute-start | bytes 147464 | tf_op jit(solution)/shard_map/ppermute | solution.py:719
  69.1 6.1 %collective-permute-start.13 = (f32[96,128]{1,0:T(8,128)S(1)}, f32[96,128]{1,0:T(8,128)S(1)}, u32[]{:S(2)}, u32[]{:S(2)}) collective-permute-start(f32[96,128]{1,0:T(8,128)S(1)} %get-tuple-element.79), channel_id=1, source_target_pairs={{0,120},{8,16},{16,8},{24,32},{32,24},{40,48},{48,40},{56,64},{64,... | collective-permute-start | bytes 147464 | tf_op jit(solution)/shard_map/ppermute | solution.py:718
  75.3 16.9 %collective-permute-start.14 = (f32[64,128]{1,0:T(8,128)S(1)}, f32[64,128]{1,0:T(8,128)S(1)}, u32[]{:S(2)}, u32[]{:S(2)}) collective-permute-start(f32[64,128]{1,0:T(8,128)S(1)} %get-tuple-element.81), channel_id=1, source_target_pairs={{0,1},{1,0},{2,3},{3,2},{4,5},{5,4},{6,7},{7,6},{8,9},{9,8},{10,11... | collective-permute-start | bytes 98312 | tf_op jit(solution)/shard_map/ppermute | solution.py:719
  75.4 16.8 %collective-permute-start.15 = (f32[64,128]{1,0:T(8,128)S(1)}, f32[64,128]{1,0:T(8,128)S(1)}, u32[]{:S(2)}, u32[]{:S(2)}) collective-permute-start(f32[64,128]{1,0:T(8,128)S(1)} %get-tuple-element.82), channel_id=1, source_target_pairs={{1,2},{2,1},{3,4},{4,3},{5,6},{6,5},{9,10},{10,9},{11,12},{12,11},... | collective-permute-start | bytes 98312 | tf_op jit(solution)/shard_map/ppermute | solution.py:718

commit v3 on v2

--- a/solution.py
+++ b/solution.py
@@ -178,6 +178,15 @@
     + ((fixed(4), 0, (1,), (0,)),)
     + FAR_PAIRS[4:]
 )
+
+
+def groups_of(planes, rows):
+    return sorted({(25 * a + 5 * b + c) // 8 for a in planes for b in rows for c in range(5)})
+
+
+INNER_GROUPS = groups_of((1, 2, 3), (0, 1, 2, 3))
+OUTER_GROUPS = groups_of((0, 4), (0, 1, 2, 3))
+LAST_GROUPS = groups_of((0, 1, 2, 3, 4), (0, 4))
 
 
 def for_blocks(count, unroll, body):
@@ -213,8 +222,7 @@
     divergence,
     balance,
     integral,
-    even_out,
-    odd_out,
+    faces,
     mixing,
     rows,
     table,
@@ -351,17 +359,13 @@
             element_rows(jnp.maximum(index - 1, 0), 3, part)
         else:
             element_rows(index, slot - 1, part)
+        if slot == 3:
+            element_rows(index, 4, part)
 
     visit_far(line_places, gather_node)
     visit_pairs(line_places, gather_node, rows_before)
 
-    def far_rows(a, carry):
-        for part in range(2):
-            element_rows(a, 4, part)
-        return carry
-
-    lax.fori_loop(0, 5, far_rows, 0)
-    for a, b in ((3, 3), (4, 0), (4, 1), (4, 2), (4, 3)):
+    for a, b in ((3, 3), (4, 0), (4, 1), (4, 2), (4, 3), (4, 4)):
         for part in range(2):
             element_rows(a, b, part)
     for point in range(125, 128):
@@ -374,7 +378,7 @@
     lame_out[0:125, :] = lame[...] * weight[0:125, :]
     lame_out[125:128, :] = jnp.zeros((3, 128), f32)
     balance_of(motion_out, force_out, 0, shear_out, lame_out, gradient, divergence, balance, integral)
-    pack_cycle(balance, blk, even_out, odd_out)
+    pack_cycle(balance, blk, faces.at[0:96, :], faces.at[96:192, :])
 
 
 def lanes_of(count):
@@ -589,15 +593,16 @@
     return step_kernel
 
 
-def scatter_to(table, state, points):
+def scatter_to(table, state, points, groups):
     def point_rows(group):
         values = jnp.concatenate(
             [state[pl.ds(group * 8 + part, 16, stride=128), :] for part in range(8)], axis=0
         )
-        start = pl.multiple_of(group * 128, 128)
+        start = group * 128
         points[pl.ds(start, 128), :] = values.T
 
-    for_blocks(16, 4, point_rows)
+    for group in groups:
+        point_rows(group)
     part_of = lanes_of(1) // 16
 
     def point_places(a, b, c):
@@ -626,7 +631,7 @@
 ):
     visit_pairs = start_pairs(numbers_hbm, chunks, sems, 3, INNER_PAIRS)
     state_of(balance, inverse, motion_in, speed_in, state)
-    visit_pairs(*scatter_to(table, state, points))
+    visit_pairs(*scatter_to(table, state, points, INNER_GROUPS))
 
 
 def outer_kernel(
@@ -645,7 +650,7 @@
     del table_in
     visit_pairs = start_pairs(numbers_hbm, chunks, sems, 1, OUTER_PAIRS)
     state_of(balance, inverse, motion_in, speed_in, state)
-    visit_pairs(*scatter_to(table, state, points))
+    visit_pairs(*scatter_to(table, state, points, OUTER_GROUPS))
 
 
 def last_kernel(
@@ -672,7 +677,7 @@
     balance[...] = old[...]
     add_lat(balance, lat, even_in, odd_in)
     state_of(balance, inverse, motion_in, speed_in, state)
-    visit_pairs(*scatter_to(table, state, points))
+    visit_pairs(*scatter_to(table, state, points, LAST_GROUPS))
 
     def turned(start):
         values = table[pl.ds(start, 128), :].T
@@ -763,8 +768,7 @@
         divergence,
         balance,
         integral,
-        even,
-        odd,
+        faces,
     ) = pl.pallas_call(
         gather_kernel,
         out_shape=(
@@ -778,11 +782,10 @@
             pltpu.VMEM((128, 1152), bf16),
             balance_shape,
             integral_shape,
-            cycle_shape,
-            cycle_shape,
+            kept(192, 128),
         ),
         in_specs=[hbm()] * 12 + [smem()],
-        out_specs=[vmem()] * 12,
+        out_specs=[vmem()] * 11,
         scratch_shapes=[
             pltpu.VMEM((24, 3 * EVENTS), f32),
             pltpu.VMEM((COMPS, NODE_BLOCKS * 128), f32),
@@ -826,6 +829,7 @@
     force, motion, speed, inverse, shear, lame, gradient, divergence = hold(
         force, motion, speed, inverse, shear, lame, gradient, divergence
     )
+    even, odd = faces[0:96], faces[96:192]
     integrals = []
     numbers_hbm = pltpu.with_memory_space_constraint(numbers, pltpu.HBM)
     table_shape = kept(NODE_BLOCKS * 128, 128)

time: 97.5 us -> 97.2 us (level)
  Pallas kernels: 34 us -> 33 us
    pallas_call x1, Pallas kernels: 14.3 us -> 13.4 us  [local(): pl.pallas_call(gather_kernel, out_shape=(kept(24 * 128, 128), kept(768, 1...]
where the time goes in v3:
time: 97.2 us; the launch traced here: 96.9 us
  starting transfers between devices  35 us (36%)
  Pallas kernels  33 us (34%)
  waiting for transfers between devices  27.2 us (28%)
  between operations  1.01 us (1%)
    ppermute x8, starting transfers between devices, exchange(): odd = lax.ppermute(odd, axis, odd_pairs)  31.5 us
    ppermute x8, waiting for transfers between devices, exchange(): odd = lax.ppermute(odd, axis, odd_pairs)  25.3 us
    pallas_call x1, Pallas kernels, local(): pl.pallas_call(gather_kernel, out_shape=(kept(24 * 128, 128), kept(768, 1...  13.4 us
    pallas_call x3, Pallas kernels, local(): pl.pallas_call(make_step_kernel(step), out_shape=(balance_shape, balance_...  5.48 us
    pallas_call x1, Pallas kernels, local(): pl.pallas_call(last_kernel, out_shape=(nodal, nodal, table_shape), in_spe...  4.79 us
    pallas_call x1, Pallas kernels, local(): pl.pallas_call(inner_kernel, out_shape=table_shape, in_specs=[hbm()] + [v...  4.38 us
    ppermute x8, starting transfers between devices, exchange(): even = lax.ppermute(even, axis, even_pairs)  3.49 us
    pallas_call x1, Pallas kernels, local(): pl.pallas_call(outer_kernel, out_shape=table_shape, in_specs=[hbm()] + [v...  2.58 us
  transfers between devices with their start and end apart: 16, of which 9 were waited for; matrix products, arithmetic and copies ran while one was open for 0% of the time, Pallas kernels for 8%

profile of v3, /device:TPU:6, one launch (start us, length us, event | category | flops | bytes accessed | tf_op | source)
XLA Modules:
  0.0 96.9 jit_solution(3517996064365515261)
XLA Ops:
  0.6 13.4 %gather.1 = (f32[3072,128]{1,0:T(8,128)S(1)}, f32[768,128]{1,0:T(8,128)S(1)}, f32[768,128]{1,0:T(8,128)S(1)}, f32[128,128]{1,0:T(8,128)S(1)}, f32[128,128]{1,0:T...) custom-call(s32[16000]{0:T(1024)} %bitcast.12, ...), custom_call_target="tpu_custom_call" | custom-call | tf_op jit(solution)/shard_map/gather/pallas_call | solution.py:772
  14.0 0.6 fusion
  14.6 0.0 collective-permute-start
  14.6 5.2 %collective-permute-start.1 = (f32[96,128]{1,0:T(8,128)}, f32[96,128]{1,0:T(8,128)}, u32[]{:S(2)}, u32[]{:S(2)}) collective-permute-start(f32[96,128]{1,0:T(8,128)} %get-tuple-element.89), channel_id=1, source_target_pairs={{0,120},{8,16},{16,8},{24,32},{32,24},{40,48},{48,40},{56,64},{64,... | collective-permute-start | bytes 147464 | tf_op jit(solution)/shard_map/ppermute | solution.py:723
  19.8 0.0 collective-permute-done.even_in
  19.8 2.1 %collective-permute-done.1.odd_in = f32[96,128]{1,0:T(8,128)} collective-permute-done((f32[96,128]{1,0:T(8,128)}, f32[96,128]{1,0:T(8,128)}, u32[]{:S(2)}, u32[]{:S(2)}) %collective-permute-start.1) | collective-permute-done | bytes 49184 | tf_op jit(solution)/shard_map/ppermute | solution.py:723
  21.9 1.0 %middle.4 = (f32[768,128]{1,0:T(8,128)S(1)}, f32[64,128]{1,0:T(8,128)S(1)}, f32[64,128]{1,0:T(8,128)S(1)}) custom-call(s32[1]{0:T(128)} %bitcast.2.blk, s32[1]{0:T(128)} %bitcast.1.lat, f32[768,128]{1,0:T(8,128)S(1)} %get-tuple-element.46.old, f32[96,128]{1,0:T(8,128)} %collective-permute-done.even_in, f32[96,128]{1,0:T(8,128)} %collective-permute-done.1.odd_in), custom_call_target="tpu_custom_call" | custom-call | tf_op jit(solution)/shard_map/middle/pallas_call | solution.py:881
  22.9 3.0 %collective-permute-start.2 = (f32[64,128]{1,0:T(8,128)S(1)}, f32[64,128]{1,0:T(8,128)S(1)}, u32[]{:S(2)}, u32[]{:S(2)}) collective-permute-start(f32[64,128]{1,0:T(8,128)S(1)} %get-tuple-element.49), channel_id=1, source_target_pairs={{0,1},{1,0},{2,3},{3,2},{4,5},{5,4},{6,7},{7,6},{8,9},{9,8},{10,11... | collective-permute-start | bytes 98312 | tf_op jit(solution)/shard_map/ppermute | solution.py:724
  25.9 2.8 %collective-permute-start.3 = (f32[64,128]{1,0:T(8,128)S(1)}, f32[64,128]{1,0:T(8,128)S(1)}, u32[]{:S(2)}, u32[]{:S(2)}) collective-permute-start(f32[64,128]{1,0:T(8,128)S(1)} %get-tuple-element.50), channel_id=1, source_target_pairs={{1,2},{2,1},{3,4},{4,3},{5,6},{6,5},{9,10},{10,9},{11,12},{12,11},... | collective-permute-start | bytes 98312 | tf_op jit(solution)/shard_map/ppermute | solution.py:723
  28.7 0.0 collective-permute-done.2.even_in
  28.7 5.4 %collective-permute-done.3.odd_in = f32[64,128]{1,0:T(8,128)S(1)} collective-permute-done((f32[64,128]{1,0:T(8,128)S(1)}, f32[64,128]{1,0:T(8,128)S(1)}, u32[]{:S(2)}, u32[]{:S(2)}) %collective-permute-start.3) | collective-permute-done | bytes 32800 | tf_op jit(solution)/shard_map/ppermute | solution.py:723
  34.1 1.8 %step.3 = (f32[768,128]{1,0:T(8,128)S(1)}, f32[768,128]{1,0:T(8,128)S(1)}, f32[768,128]{1,0:T(8,128)S(1)}, f32[10,128]{1,0:T(8,128)S(1)}, f32[96,128]{1,0:T(8,128)S(1)}, /*index=5*/f32[96,128]{1,0:T(8,128)S(1)}) custom-call(s32[1]{0:T(128)} %bitcast.2.blk, s32[1]{0:T(128)} %bitcast.1.lat, f32[768,128]{1,0:T(8,128)S(1)} %get-tuple-element.48.old, ...), custom_call_target="tpu_custom_call" | custom-call | tf_op jit(solution)/shard_map/step/pallas_call | solution.py:839
  35.9 0.1 collective-permute-start.4
  36.0 2.0 %collective-permute-start.5 = (f32[96,128]{1,0:T(8,128)S(1)}, f32[96,128]{1,0:T(8,128)S(1)}, u32[]{:S(2)}, u32[]{:S(2)}) collective-permute-start(f32[96,128]{1,0:T(8,128)S(1)} %get-tuple-element.61), channel_id=1, source_target_pairs={{0,120},{8,16},{16,8},{24,32},{32,24},{40,48},{48,40},{56,64},{64,... | collective-permute-start | bytes 147464 | tf_op jit(solution)/shard_map/ppermute | solution.py:723
  38.0 0.0 collective-permute-done.4.even_in
  38.0 4.2 %collective-permute-done.5.odd_in = f32[96,128]{1,0:T(8,128)S(1)} collective-permute-done((f32[96,128]{1,0:T(8,128)S(1)}, f32[96,128]{1,0:T(8,128)S(1)}, u32[]{:S(2)}, u32[]{:S(2)}) %collective-permute-start.5) | collective-permute-done | bytes 49184 | tf_op jit(solution)/shard_map/ppermute | solution.py:723
  42.1 0.2 middle.5
  42.3 0.1 collective-permute-start.6
  42.4 5.7 %collective-permute-start.7 = (f32[64,128]{1,0:T(8,128)S(1)}, f32[64,128]{1,0:T(8,128)S(1)}, u32[]{:S(2)}, u32[]{:S(2)}) collective-permute-start(f32[64,128]{1,0:T(8,128)S(1)} %get-tuple-element.64), channel_id=1, source_target_pairs={{1,2},{2,1},{3,4},{4,3},{5,6},{6,5},{9,10},{10,9},{11,12},{12,11},... | collective-permute-start | bytes 98312 | tf_op jit(solution)/shard_map/ppermute | solution.py:723
  48.1 0.0 collective-permute-done.6.even_in
  48.1 2.5 %collective-permute-done.7.odd_in = f32[64,128]{1,0:T(8,128)S(1)} collective-permute-done((f32[64,128]{1,0:T(8,128)S(1)}, f32[64,128]{1,0:T(8,128)S(1)}, u32[]{:S(2)}, u32[]{:S(2)}) %collective-permute-start.7) | collective-permute-done | bytes 32800 | tf_op jit(solution)/shard_map/ppermute | solution.py:723
  50.6 1.8 %step.4 = (f32[768,128]{1,0:T(8,128)S(1)}, f32[768,128]{1,0:T(8,128)S(1)}, f32[768,128]{1,0:T(8,128)S(1)}, f32[10,128]{1,0:T(8,128)S(1)}, f32[96,128]{1,0:T(8,128)S(1)}, /*index=5*/f32[96,128]{1,0:T(8,128)S(1)}) custom-call(s32[1]{0:T(128)} %bitcast.2.blk, s32[1]{0:T(128)} %bitcast.1.lat, f32[768,128]{1,0:T(8,128)S(1)} %get-tuple-element.62.old, ...), custom_call_target="tpu_custom_call" | custom-call | tf_op jit(solution)/shard_map/step/pallas_call | solution.py:839
  52.4 0.1 collective-permute-start.8
  52.5 0.4 collective-permute-start.9
  52.9 0.8 collective-permute-done.8.even_in
  53.8 4.5 %collective-permute-done.9.odd_in = f32[96,128]{1,0:T(8,128)S(1)} collective-permute-done((f32[96,128]{1,0:T(8,128)S(1)}, f32[96,128]{1,0:T(8,128)S(1)}, u32[]{:S(2)}, u32[]{:S(2)}) %collective-permute-start.9) | collective-permute-done | bytes 49184 | tf_op jit(solution)/shard_map/ppermute | solution.py:723
  58.2 0.2 middle.6
  58.4 0.1 collective-permute-start.10
  58.5 6.3 %collective-permute-start.11 = (f32[64,128]{1,0:T(8,128)S(1)}, f32[64,128]{1,0:T(8,128)S(1)}, u32[]{:S(2)}, u32[]{:S(2)}) collective-permute-start(f32[64,128]{1,0:T(8,128)S(1)} %get-tuple-element.72), channel_id=1, source_target_pairs={{1,2},{2,1},{3,4},{4,3},{5,6},{6,5},{9,10},{10,9},{11,12},{12,11},... | collective-permute-start | bytes 98312 | tf_op jit(solution)/shard_map/ppermute | solution.py:723
  64.9 0.0 collective-permute-done.10.even_in
  64.9 1.8 %collective-permute-done.11.odd_in = f32[64,128]{1,0:T(8,128)S(1)} collective-permute-done((f32[64,128]{1,0:T(8,128)S(1)}, f32[64,128]{1,0:T(8,128)S(1)}, u32[]{:S(2)}, u32[]{:S(2)}) %collective-permute-start.11) | collective-permute-done | bytes 32800 | tf_op jit(solution)/shard_map/ppermute | solution.py:723
  66.7 0.0 copy-start
  66.7 1.8 %step.5 = (f32[768,128]{1,0:T(8,128)S(1)}, f32[768,128]{1,0:T(8,128)S(1)}, f32[768,128]{1,0:T(8,128)S(1)}, f32[10,128]{1,0:T(8,128)S(1)}, f32[96,128]{1,0:T(8,128)S(1)}, /*index=5*/f32[96,128]{1,0:T(8,128)S(1)}) custom-call(s32[1]{0:T(128)} %bitcast.2.blk, s32[1]{0:T(128)} %bitcast.1.lat, f32[768,128]{1,0:T(8,128)S(1)} %get-tuple-element.70.old, ...), custom_call_target="tpu_custom_call" | custom-call | tf_op jit(solution)/shard_map/step/pallas_call | solution.py:839
  68.6 0.1 collective-permute-start.12
  68.7 0.1 collective-permute-start.13
  68.7 1.1 %collective-permute-done.12.even_in = f32[96,128]{1,0:T(8,128)S(1)} collective-permute-done((f32[96,128]{1,0:T(8,128)S(1)}, f32[96,128]{1,0:T(8,128)S(1)}, u32[]{:S(2)}, u32[]{:S(2)}) %collective-permute-start.12) | collective-permute-done | bytes 49184 | tf_op jit(solution)/shard_map/ppermute | solution.py:724
  69.9 4.8 %collective-permute-done.13.odd_in = f32[96,128]{1,0:T(8,128)S(1)} collective-permute-done((f32[96,128]{1,0:T(8,128)S(1)}, f32[96,128]{1,0:T(8,128)S(1)}, u32[]{:S(2)}, u32[]{:S(2)}) %collective-permute-start.13) | collective-permute-done | bytes 49184 | tf_op jit(solution)/shard_map/ppermute | solution.py:723
  74.6 0.2 middle.7
  74.8 0.1 collective-permute-start.14
  74.9 9.1 %collective-permute-start.15 = (f32[64,128]{1,0:T(8,128)S(1)}, f32[64,128]{1,0:T(8,128)S(1)}, u32[]{:S(2)}, u32[]{:S(2)}) collective-permute-start(f32[64,128]{1,0:T(8,128)S(1)} %get-tuple-element.80), channel_id=1, source_target_pairs={{1,2},{2,1},{3,4},{4,3},{5,6},{6,5},{9,10},{10,9},{11,12},{12,11},... | collective-permute-start | bytes 98312 | tf_op jit(solution)/shard_map/ppermute | solution.py:723
  84.0 4.4 %inner.1.table_in = f32[9984,128]{1,0:T(8,128)S(1)} custom-call(s32[16000]{0:T(1024)} %bitcast.13, f32[768,128]{1,0:T(8,128)S(1)} %get-tuple-element.75.old.balance, f32[128,128]{1,0:T(8,128)S(1)} %get-tuple-element.51.inverse, f32[768,128]{1,0:T(8,128)S(1)} %get-tuple-element.81.motion_in, f32[768,128]{1,0:T(8,128)S(1)} %get-tuple-element.82.speed_in), custom_call_target="tpu_custom_call" | custom-call | tf_op jit(solution)/shard_map/inner/pallas_call | solution.py:872
  88.4 0.0 copy-done
  88.4 0.9 spectrum.1
  89.3 2.6 %outer.1.table_in = f32[9984,128]{1,0:T(8,128)S(1)} custom-call(s32[16000]{0:T(1024)} %bitcast.14, f32[768,128]{1,0:T(8,128)S(1)} %get-tuple-element.78.balance.old, f32[128,128]{1,0:T(8,128)S(1)} %get-tuple-element.51.inverse, f32[768,128]{1,0:T(8,128)S(1)} %get-tuple-element.81.motion_in, ...), custom_call_target="tpu_custom_call", output_to_operand_aliasing={{}: (5, {})} | custom-call | tf_op jit(solution)/shard_map/outer/pallas_call | solution.py:891
  91.9 0.0 collective-permute-done.14.even_in
  91.9 0.0 collective-permute-done.15.odd_in
  91.9 4.8 %last.1 = (f32[3,2,9945]{2,1,0:T(2,128)}, f32[3,2,9945]{2,1,0:T(2,128)}, f32[9984,128]{1,0:T(8,128)S(1)}) custom-call(s32[16000]{0:T(1024)} %bitcast.15, s32[1]{0:T(128)} %bitcast.1.lat, f32[768,128]{1,0:T(8,128)S(1)} %get-tuple-element.78.balance.old, f32[64,128]{1,0:T(8,128)S(1)} %collective-permute-done.14.even_in, ...), custom_call_target="tpu_custom_call", output_to_operand_aliasing={{2}: (8, {})} | custom-call | tf_op jit(solution)/shard_map/last/pallas_call | solution.py:910
Async XLA Ops:
  14.6 5.2 %collective-permute-start = (f32[96,128]{1,0:T(8,128)}, f32[96,128]{1,0:T(8,128)}, u32[]{:S(2)}, u32[]{:S(2)}) collective-permute-start(f32[96,128]{1,0:T(8,128)} %get-tuple-element.90), channel_id=1, source_target_pairs={{0,8},{8,0},{16,24},{24,16},{32,40},{40,32},{48,56},{56,48},{64,72... | collective-permute-start | bytes 147464 | tf_op jit(solution)/shard_map/ppermute | solution.py:724
  14.6 7.3 %collective-permute-start.1 = (f32[96,128]{1,0:T(8,128)}, f32[96,128]{1,0:T(8,128)}, u32[]{:S(2)}, u32[]{:S(2)}) collective-permute-start(f32[96,128]{1,0:T(8,128)} %get-tuple-element.89), channel_id=1, source_target_pairs={{0,120},{8,16},{16,8},{24,32},{32,24},{40,48},{48,40},{56,64},{64,... | collective-permute-start | bytes 147464 | tf_op jit(solution)/shard_map/ppermute | solution.py:723
  22.9 5.8 %collective-permute-start.2 = (f32[64,128]{1,0:T(8,128)S(1)}, f32[64,128]{1,0:T(8,128)S(1)}, u32[]{:S(2)}, u32[]{:S(2)}) collective-permute-start(f32[64,128]{1,0:T(8,128)S(1)} %get-tuple-element.49), channel_id=1, source_target_pairs={{0,1},{1,0},{2,3},{3,2},{4,5},{5,4},{6,7},{7,6},{8,9},{9,8},{10,11... | collective-permute-start | bytes 98312 | tf_op jit(solution)/shard_map/ppermute | solution.py:724
  25.9 8.2 %collective-permute-start.3 = (f32[64,128]{1,0:T(8,128)S(1)}, f32[64,128]{1,0:T(8,128)S(1)}, u32[]{:S(2)}, u32[]{:S(2)}) collective-permute-start(f32[64,128]{1,0:T(8,128)S(1)} %get-tuple-element.50), channel_id=1, source_target_pairs={{1,2},{2,1},{3,4},{4,3},{5,6},{6,5},{9,10},{10,9},{11,12},{12,11},... | collective-permute-start | bytes 98312 | tf_op jit(solution)/shard_map/ppermute | solution.py:723
  35.9 2.1 %collective-permute-start.4 = (f32[96,128]{1,0:T(8,128)S(1)}, f32[96,128]{1,0:T(8,128)S(1)}, u32[]{:S(2)}, u32[]{:S(2)}) collective-permute-start(f32[96,128]{1,0:T(8,128)S(1)} %get-tuple-element.60), channel_id=1, source_target_pairs={{0,8},{8,0},{16,24},{24,16},{32,40},{40,32},{48,56},{56,48},{64,72... | collective-permute-start | bytes 147464 | tf_op jit(solution)/shard_map/ppermute | solution.py:724
  36.0 6.1 %collective-permute-start.5 = (f32[96,128]{1,0:T(8,128)S(1)}, f32[96,128]{1,0:T(8,128)S(1)}, u32[]{:S(2)}, u32[]{:S(2)}) collective-permute-start(f32[96,128]{1,0:T(8,128)S(1)} %get-tuple-element.61), channel_id=1, source_target_pairs={{0,120},{8,16},{16,8},{24,32},{32,24},{40,48},{48,40},{56,64},{64,... | collective-permute-start | bytes 147464 | tf_op jit(solution)/shard_map/ppermute | solution.py:723
  42.3 5.8 %collective-permute-start.6 = (f32[64,128]{1,0:T(8,128)S(1)}, f32[64,128]{1,0:T(8,128)S(1)}, u32[]{:S(2)}, u32[]{:S(2)}) collective-permute-start(f32[64,128]{1,0:T(8,128)S(1)} %get-tuple-element.63), channel_id=1, source_target_pairs={{0,1},{1,0},{2,3},{3,2},{4,5},{5,4},{6,7},{7,6},{8,9},{9,8},{10,11... | collective-permute-start | bytes 98312 | tf_op jit(solution)/shard_map/ppermute | solution.py:724
  42.4 8.2 %collective-permute-start.7 = (f32[64,128]{1,0:T(8,128)S(1)}, f32[64,128]{1,0:T(8,128)S(1)}, u32[]{:S(2)}, u32[]{:S(2)}) collective-permute-start(f32[64,128]{1,0:T(8,128)S(1)} %get-tuple-element.64), channel_id=1, source_target_pairs={{1,2},{2,1},{3,4},{4,3},{5,6},{6,5},{9,10},{10,9},{11,12},{12,11},... | collective-permute-start | bytes 98312 | tf_op jit(solution)/shard_map/ppermute | solution.py:723
  52.4 1.3 %collective-permute-start.8 = (f32[96,128]{1,0:T(8,128)S(1)}, f32[96,128]{1,0:T(8,128)S(1)}, u32[]{:S(2)}, u32[]{:S(2)}) collective-permute-start(f32[96,128]{1,0:T(8,128)S(1)} %get-tuple-element.68), channel_id=1, source_target_pairs={{0,8},{8,0},{16,24},{24,16},{32,40},{40,32},{48,56},{56,48},{64,72... | collective-permute-start | bytes 147464 | tf_op jit(solution)/shard_map/ppermute | solution.py:724
  52.5 5.7 %collective-permute-start.9 = (f32[96,128]{1,0:T(8,128)S(1)}, f32[96,128]{1,0:T(8,128)S(1)}, u32[]{:S(2)}, u32[]{:S(2)}) collective-permute-start(f32[96,128]{1,0:T(8,128)S(1)} %get-tuple-element.69), channel_id=1, source_target_pairs={{0,120},{8,16},{16,8},{24,32},{32,24},{40,48},{48,40},{56,64},{64,... | collective-permute-start | bytes 147464 | tf_op jit(solution)/shard_map/ppermute | solution.py:723
  58.4 6.4 %collective-permute-start.10 = (f32[64,128]{1,0:T(8,128)S(1)}, f32[64,128]{1,0:T(8,128)S(1)}, u32[]{:S(2)}, u32[]{:S(2)}) collective-permute-start(f32[64,128]{1,0:T(8,128)S(1)} %get-tuple-element.71), channel_id=1, source_target_pairs={{0,1},{1,0},{2,3},{3,2},{4,5},{5,4},{6,7},{7,6},{8,9},{9,8},{10,11... | collective-permute-start | bytes 98312 | tf_op jit(solution)/shard_map/ppermute | solution.py:724
  58.5 8.2 %collective-permute-start.11 = (f32[64,128]{1,0:T(8,128)S(1)}, f32[64,128]{1,0:T(8,128)S(1)}, u32[]{:S(2)}, u32[]{:S(2)}) collective-permute-start(f32[64,128]{1,0:T(8,128)S(1)} %get-tuple-element.72), channel_id=1, source_target_pairs={{1,2},{2,1},{3,4},{4,3},{5,6},{6,5},{9,10},{10,9},{11,12},{12,11},... | collective-permute-start | bytes 98312 | tf_op jit(solution)/shard_map/ppermute | solution.py:723
  66.7 21.7 %copy-start = (bf16[640,128]{1,0:T(8,128)(2,1)S(1)}, bf16[640,128]{1,0:T(8,128)(2,1)}, u32[]{:S(2)}) copy-start(bf16[640,128]{1,0:T(8,128)(2,1)} %constant.23.clone.wide) | copy-start | bytes 491524
  68.6 1.3 %collective-permute-start.12 = (f32[96,128]{1,0:T(8,128)S(1)}, f32[96,128]{1,0:T(8,128)S(1)}, u32[]{:S(2)}, u32[]{:S(2)}) collective-permute-start(f32[96,128]{1,0:T(8,128)S(1)} %get-tuple-element.76), channel_id=1, source_target_pairs={{0,8},{8,0},{16,24},{24,16},{32,40},{40,32},{48,56},{56,48},{64,72... | collective-permute-start | bytes 147464 | tf_op jit(solution)/shard_map/ppermute | solution.py:724
  68.7 6.0 %collective-permute-start.13 = (f32[96,128]{1,0:T(8,128)S(1)}, f32[96,128]{1,0:T(8,128)S(1)}, u32[]{:S(2)}, u32[]{:S(2)}) collective-permute-start(f32[96,128]{1,0:T(8,128)S(1)} %get-tuple-element.77), channel_id=1, source_target_pairs={{0,120},{8,16},{16,8},{24,32},{32,24},{40,48},{48,40},{56,64},{64,... | collective-permute-start | bytes 147464 | tf_op jit(solution)/shard_map/ppermute | solution.py:723
  74.8 17.1 %collective-permute-start.14 = (f32[64,128]{1,0:T(8,128)S(1)}, f32[64,128]{1,0:T(8,128)S(1)}, u32[]{:S(2)}, u32[]{:S(2)}) collective-permute-start(f32[64,128]{1,0:T(8,128)S(1)} %get-tuple-element.79), channel_id=1, source_target_pairs={{0,1},{1,0},{2,3},{3,2},{4,5},{5,4},{6,7},{7,6},{8,9},{9,8},{10,11... | collective-permute-start | bytes 98312 | tf_op jit(solution)/shard_map/ppermute | solution.py:724
  74.9 17.0 %collective-permute-start.15 = (f32[64,128]{1,0:T(8,128)S(1)}, f32[64,128]{1,0:T(8,128)S(1)}, u32[]{:S(2)}, u32[]{:S(2)}) collective-permute-start(f32[64,128]{1,0:T(8,128)S(1)} %get-tuple-element.80), channel_id=1, source_target_pairs={{1,2},{2,1},{3,4},{4,3},{5,6},{6,5},{9,10},{10,9},{11,12},{12,11},... | collective-permute-start | bytes 98312 | tf_op jit(solution)/shard_map/ppermute | solution.py:723
